TPU v7x, 128 devices: a whole 4x4x4 slice. The times are simulated.
128 devices in a mesh: req: 16 (over x, z), tile: 8 (over y, core).
Axes of the slice: x: 4, y: 4, z: 4, core: 2. Of those that a mesh axis runs over, the one named last changes fastest.
Arguments:
- latents: bfloat16 [1024, 16, 128], P(('req', 'tile')), may hold values from -6 to 6
- piece_dest: int32 [1024], replicated, may hold values from 0 to 1023, as said below
- frames: int32 [16], replicated, may hold values from 1 to 2
- heights: int32 [16], replicated, may hold values from 16 to 32
- widths: int32 [16], replicated, may hold values from 64 to 128
- w_in: bfloat16 [3, 3, 3, 384, 16], replicated, may hold values from -0.3125 to 0.3125
- b_in: float32 [384], replicated, may hold values from -3 to 3
- gain_norm: float32 [384], replicated, may hold values from 0.5 to 1.5
- w_res: bfloat16 [3, 3, 3, 384, 384], replicated, may hold values from -0.0625 to 0.0625
- b_res: float32 [384], replicated, may hold values from -3 to 3
- w_time: bfloat16 [3, 768, 384], replicated, may hold values from -0.1875 to 0.1875
- b_time: float32 [768], replicated, may hold values from -3 to 3
- w_up: bfloat16 [3, 3, 192, 384], replicated, may hold values from -0.109375 to 0.109375
- b_up: float32 [192], replicated, may hold values from -3 to 3
Outputs:
- decoded: bfloat16 [16, 192, 4, 64, 256], P('req', None, None, 'tile')
Inputs may be any that keep to these rules, and one draw needn't show every extreme that they name: piece_dest is a permutation of the decoder slots. Requests are packed one after another in a drawn order, each request's rows frame after frame and row after row, so the 8 rows of one device are consecutive rows of one request and no device sends more than 4 rows to one device.
All inputs are finite; a program needn't handle non-finite values.
Results may differ from a plain program's by a relative error of at most 0.0075.
Values may be sent and summed in bfloat16 or wider, within the bound.
No kernel may reach another device: no remote copies, remote signals or barrier semaphores. Data moves between devices by JAX's collectives and lax.ppermute only.
A program may use at most 192 MiB of HBM per device.

v0:
```python
import jax
import jax.numpy as jnp
from jax import lax
from jax.sharding import PartitionSpec as P

LFRAMES = 2


def with_halo(cells, sides, width):
    for axis, dim in sides:
        count = lax.axis_size(axis)
        ends = count - 1
        head = lax.slice_in_dim(cells, 0, width, axis=dim)
        tail = lax.slice_in_dim(cells, cells.shape[dim] - width, cells.shape[dim], axis=dim)
        cells = jnp.concatenate(
            [
                lax.ppermute(tail, axis, [(i, (i + 1) % count) for i in range(ends)]),
                cells,
                lax.ppermute(head, axis, [((i + 1) % count, i) for i in range(ends)]),
            ],
            axis=dim,
        )
    return cells


def causal_conv(extended, weight, offsets):
    frame_count = extended.shape[1]
    row_count = extended.shape[2] - 2
    col_count = extended.shape[3]
    padded = jnp.pad(extended, ((0, 0), (2, 0), (0, 0), (1, 1)))
    shifted = jnp.stack([padded[..., tap_c : tap_c + col_count] for tap_c in range(3)], axis=0)
    summed = jnp.zeros((weight.shape[3], frame_count, row_count, col_count), jnp.float32)
    for tap_t in range(3):
        for tap_r in range(3):
            kernel = jnp.transpose(weight[tap_t, tap_r], (1, 0, 2))
            summed = summed + jnp.einsum(
                "okc,kcthw->othw",
                kernel,
                shifted[:, :, tap_t : tap_t + frame_count, tap_r : tap_r + row_count, :],
                preferred_element_type=jnp.float32,
            )
    return summed + offsets[:, None, None, None]


def time_double(features, cell_mask, w_time, b_time):
    channels, frame_count = (features.shape[0], features.shape[1])
    padded = jnp.pad(features, ((0, 0), (2, 0), (0, 0), (0, 0)))
    twice = jnp.zeros((2 * channels,) + features.shape[1:], jnp.float32)
    for tap_t in range(3):
        twice = twice + jnp.einsum(
            "oc,cthw->othw",
            w_time[tap_t],
            padded[:, tap_t : tap_t + frame_count],
            preferred_element_type=jnp.float32,
        )
    twice = twice + b_time[:, None, None, None]
    doubled = jnp.stack([twice[:channels], twice[channels:]], axis=2)
    doubled = doubled.reshape((channels, 2 * frame_count) + features.shape[2:])
    return (doubled * jnp.repeat(cell_mask, 2, axis=0)).astype(jnp.bfloat16)


def on_device(
    latents,
    piece_dest,
    frames,
    heights,
    widths,
    w_in,
    b_in,
    gain_norm,
    w_res,
    b_res,
    w_time,
    b_time,
    w_up,
    b_up,
):
    tile_count = lax.axis_size("tile")
    group_id = lax.axis_index("req")
    tile_id = lax.axis_index("tile")
    device_id = group_id * tile_count + tile_id
    slot_count, channels, col_count = latents.shape
    rows_dev = slot_count // LFRAMES
    flattened = latents.reshape(slot_count, channels * col_count)
    wanted = device_id * slot_count + jnp.arange(slot_count, dtype=jnp.int32)
    selector = (piece_dest[None, :] == wanted[:, None]).astype(jnp.bfloat16)
    latent_grid = jnp.dot(
        selector,
        lax.all_gather(flattened, ("req", "tile"), axis=0, tiled=True),
        preferred_element_type=jnp.float32,
    )
    latent_grid = latent_grid.reshape(LFRAMES, rows_dev, channels, col_count).transpose(2, 0, 1, 3)
    frame_ids = jnp.arange(LFRAMES, dtype=jnp.int32)
    row_ids = tile_id * rows_dev - 1 + jnp.arange(rows_dev + 2, dtype=jnp.int32)
    col_ids = jnp.arange(col_count, dtype=jnp.int32)
    mask_extended = (
        (frame_ids < frames[group_id])[:, None, None]
        & ((row_ids >= 0) & (row_ids < heights[group_id]))[None, :, None]
        & (col_ids < widths[group_id])[None, None, :]
    ).astype(jnp.float32)
    mask_core = mask_extended[:, 1:-1, :]
    masked_input = (latent_grid * mask_core).astype(jnp.bfloat16)
    input_rim = with_halo(masked_input, (("tile", 2),), 1)
    first = causal_conv(input_rim, w_in, b_in).astype(jnp.bfloat16)
    first_f = first.astype(jnp.float32)
    scaled = (
        first_f
        * lax.rsqrt(jnp.mean(first_f * first_f, axis=0, keepdims=True) + 1e-06)
        * gain_norm[:, None, None, None]
    )
    normed = (jax.nn.silu(scaled) * mask_core).astype(jnp.bfloat16)
    normed_rim = with_halo(normed, (("tile", 2),), 1)
    block = (first_f + causal_conv(normed_rim, w_res, b_res)).astype(jnp.bfloat16)
    timed = time_double(block, mask_core, w_time, b_time)
    timed_rim = with_halo(timed, (("tile", 2),), 1)
    out_rows = 2 * rows_dev
    out_cols = 2 * col_count
    taller = jnp.repeat(timed_rim, 2, axis=2)[:, :, 1:-1, :]
    widened = jnp.repeat(taller, 2, axis=3)
    padded = jnp.pad(widened, ((0, 0), (0, 0), (0, 0), (1, 1)))
    shifted = jnp.stack([padded[..., tap_c : tap_c + out_cols] for tap_c in range(3)], axis=0)
    summed = jnp.zeros((w_up.shape[2], timed_rim.shape[1], out_rows, out_cols), jnp.float32)
    for tap_r in range(3):
        kernel = jnp.transpose(w_up[tap_r], (1, 0, 2))
        summed = summed + jnp.einsum(
            "okc,kcthw->othw",
            kernel,
            shifted[:, :, :, tap_r : tap_r + out_rows, :],
            preferred_element_type=jnp.float32,
        )
    summed = summed + b_up[:, None, None, None]
    out_mask = jnp.repeat(jnp.repeat(jnp.repeat(mask_core, 2, axis=0), 2, axis=1), 2, axis=2)
    decoded = (summed * out_mask).astype(jnp.bfloat16)
    return decoded[None]


def solution(mesh):
    return jax.shard_map(
        on_device,
        mesh=mesh,
        in_specs=(
            P(("req", "tile"), None, None),
            P(),
            P(),
            P(),
            P(),
            P(),
            P(),
            P(),
            P(),
            P(),
            P(),
            P(),
            P(),
            P(),
        ),
        out_specs=P("req", None, None, "tile", None),
        check_vma=False,
    )
```

profile of v0, /device:TPU:8, one launch (start us, length us, event | category | flops | bytes accessed | tf_op | source)
XLA Modules:
  0.0 274.1 jit_solution(13141081143045550669)
XLA Ops:
  14.1 64.0 %all-gather.2.cloned.1.call-done = bf16[1024,2048]{1,0:T(8,128)(2,1)} async-done(((bf16[8,2048]{1,0:T(8,128)(2,1)}), bf16[1024,2048]{1,0:T(8,128)(2,1)}) %all-gather.2.cloned.1.call-update) | async-done | bytes 4194320 | tf_op jit(solution)/shard_map/all_gather | solution.py:89
  78.1 2.9 %convolution_bitcast_fusion = f32[1,8,16,128]{3,1,2,0:T(8,128)S(1)} fusion(bf16[1024,2048]{1,0:T(8,128)(2,1)} %all-gather.2.cloned.1.call-done, s32[1024]{0:T(1024)} %param.15, s32[8]{0:T(128)S(1)} %iota_add_fusion), kind=kOutput, calls=%fused_computation.101 | convolution fusion | flops 33562624 | bytes 4263968 | tf_op jit(solution)/shard_map/dot_general | solution.py:87
  83.2 3.4 %collective-permute-start.1 = (bf16[16,2,1,128]{3,0,2,1:T(8,128)(2,1)S(1)}, bf16[16,2,1,128]{3,0,2,1:T(8,128)(2,1)S(1)}, u32[]{:S(2)}, u32[]{:S(2)}) collective-permute-start(bf16[16,2,1,128]{3,0,2,1:T(8,128)(2,1)S(1)} %get-tuple-element.29), channel_id=1, source_target_pairs={{1,0},{2,1},{3,2},{4,3},{5,4},{6,5},{7,6},{9,8},{10,9},{11,10},{12... | collective-permute-start | bytes 24584 | tf_op jit(solution)/shard_map/ppermute | solution.py:19
  93.1 3.2 %collective-permute-start.2 = (bf16[384,2,1,128]{0,3,2,1:T(8,128)(2,1)S(1)}, bf16[384,2,1,128]{0,3,2,1:T(8,128)(2,1)S(1)}, u32[]{:S(2)}, u32[]{:S(2)}) collective-permute-start(bf16[384,2,1,128]{0,3,2,1:T(8,128)(2,1)S(1)} %get-tuple-element.23), channel_id=1, source_target_pairs={{0,1},{1,2},{2,3},{3,4},{4,5},{5,6},{6,7},{8,9},{9,10},{10,11},{11... | collective-permute-start | bytes 589832 | tf_op jit(solution)/shard_map/ppermute | solution.py:17
  96.3 2.4 collective-permute-start.3
  106.8 8.3 %fusion.160 = (bf16[3,384,2,4,128]{1,4,3,2,0:T(8,128)(2,1)}, bf16[3,384,2,4,128]{1,4,3,2,0:T(8,128)(2,1)}, bf16[3,384,2,4,128]{1,4,3,2,0:T(8,128)(2,1)}, bf16[3,...) fusion(bf16[3,384,4,6,128]{1,4,3,2,0:T(8,128)(2,1)S(1)} %pad_ma, ...), kind=kLoop, calls=%fused_computation.194 | loop fusion | bytes 42467328 | tf_op jit(solution)/shard_map/slice | solution.py:39
  115.2 3.5 %fusion.57 = f32[2,4,128,384]{3,2,0,1:T(8,128)S(1)} fusion(bf16[3,384,2,4,128]{1,4,3,2,0:T(8,128)(2,1)} %get-tuple-element.7, bf16[3,3,3,384,384]{4,3,2,1,0:T(8,128)(2,1)} %param.22), kind=kOutput, calls=%fused_computation.92 | convolution fusion | flops 905969664 | bytes 4816896 | tf_op jit(solution)/shard_map/okc,kcthw->othw/dot_general | solution.py:36
  118.7 2.8 %fusion.60 = f32[2,4,128,384]{3,2,0,1:T(8,128)S(1)} fusion(bf16[3,384,2,4,128]{1,4,3,2,0:T(8,128)(2,1)S(1)} %copy-done.9, bf16[3,3,3,384,384]{4,3,2,1,0:T(8,128)(2,1)} %param.22), kind=kOutput, calls=%fused_computation.93 | convolution fusion | flops 905969664 | bytes 4816896 | tf_op jit(solution)/shard_map/okc,kcthw->othw/dot_general | solution.py:36
  121.5 2.8 %fusion.63 = f32[2,4,128,384]{3,2,0,1:T(8,128)S(1)} fusion(bf16[3,384,2,4,128]{1,4,3,2,0:T(8,128)(2,1)S(1)} %copy-done.8, bf16[3,3,3,384,384]{4,3,2,1,0:T(8,128)(2,1)} %param.22), kind=kOutput, calls=%fused_computation.94 | convolution fusion | flops 905969664 | bytes 4816896 | tf_op jit(solution)/shard_map/okc,kcthw->othw/dot_general | solution.py:36
  124.3 2.8 %fusion.66 = f32[2,4,128,384]{3,2,0,1:T(8,128)S(1)} fusion(bf16[3,384,2,4,128]{1,4,3,2,0:T(8,128)(2,1)S(1)} %copy-done.7, bf16[3,3,3,384,384]{4,3,2,1,0:T(8,128)(2,1)} %param.22), kind=kOutput, calls=%fused_computation.95 | convolution fusion | flops 905969664 | bytes 4816896 | tf_op jit(solution)/shard_map/okc,kcthw->othw/dot_general | solution.py:36
  141.1 2.4 copy.67
  145.8 3.5 %collective-permute-start.4 = (bf16[384,4,1,128]{3,0,2,1:T(8,128)(2,1)}, bf16[384,4,1,128]{3,0,2,1:T(8,128)(2,1)S(1)}, u32[]{:S(2)}, u32[]{:S(2)}) collective-permute-start(bf16[384,4,1,128]{3,0,2,1:T(8,128)(2,1)} %get-tuple-element.21), channel_id=1, source_target_pairs={{0,1},{1,2},{2,3},{3,4},{4,5},{5,6},{6,7},{8,9},{9,10},{10,11},{11... | collective-permute-start | bytes 1179656 | tf_op jit(solution)/shard_map/ppermute | solution.py:17
  149.3 2.6 collective-permute-start.5
  153.0 2.4 collective-permute-done.4
  158.6 4.1 %copy.68 = bf16[384,4,6,128]{0,1,3,2:T(4,128)(2,1)S(1)} copy(bf16[384,4,6,128]{3,0,2,1:T(8,128)(2,1)} %pad_maximum_fusion.3) | data formatting | bytes 4718592 | tf_op jit(solution)/shard_map/concatenate | solution.py:15
  166.1 4.1 %broadcast_in_dim.14 = bf16[384,4,10,128,2]{0,1,4,3,2:T(4,128)(2,1)} broadcast(bf16[384,4,10,128]{0,1,3,2:T(4,128)(2,1)S(1)} %slice.290), dimensions={0,1,2,3} | broadcast | bytes 11796480 | tf_op jit(solution)/shard_map/broadcast_in_dim | solution.py:119
  170.2 13.1 %copy.69 = bf16[384,4,10,256]{3,0,2,1:T(8,128)(2,1)} copy(bf16[384,4,10,256]{0,1,3,2:T(4,128)(2,1)} %bitcast.377) | data formatting | bytes 15728640 | tf_op jit(solution)/shard_map/reshape | solution.py:119
  183.3 14.4 %fusion.6 = (bf16[1,384,4,10,256]{4,1,0,3,2:T(8,128)(2,1)}, bf16[1,384,4,10,256]{4,1,0,3,2:T(8,128)(2,1)}) fusion(bf16[384,4,10,256]{3,0,2,1:T(8,128)(2,1)} %copy.69), kind=kLoop, calls=%fused_computation.9 | loop fusion | bytes 23592960 | tf_op jit(solution)/shard_map/stack | solution.py:121
  197.7 13.1 %copy.71 = bf16[1,384,4,10,256]{4,1,0,3,2:T(8,128)(2,1)} copy(bf16[1,384,4,10,256]{1,2,4,3,0:T(4,128)(2,1)} %bitcast.378) | data formatting | bytes 15728640 | tf_op jit(solution)/shard_map/stack | solution.py:121
  210.7 19.9 %pad_maximum_fusion = bf16[3,384,4,10,256]{4,1,0,3,2:T(8,128)(2,1)} fusion(bf16[1,384,4,10,256]{4,1,0,3,2:T(8,128)(2,1)} %get-tuple-element.6, bf16[1,384,4,10,256]{4,1,0,3,2:T(8,128)(2,1)} %copy.71, bf16[1,384,4,10,256]{4,1,0,3,2:T(8,128)(2,1)} %get-tuple-element.5), kind=kLoop, calls=%fused_computation | loop fusion | flops 23592960 | bytes 47185920 | tf_op jit(solution)/shard_map/stack | solution.py:121
  230.6 10.3 %fusion = f32[4,8,256,192,1]{2,3,4,1,0:T(8,128)} fusion(bf16[3,384,4,10,256]{4,1,0,3,2:T(8,128)(2,1)} %pad_maximum_fusion, bf16[3,3,192,384]{3,2,1,0:T(8,128)(2,1)S(1)} %copy-done.17), kind=kOutput, calls=%fused_computation.1 | convolution fusion | flops 3623878656 | bytes 25608192 | tf_op jit(solution)/shard_map/okc,kcthw->othw/dot_general | solution.py:125
  241.0 10.4 %fusion.2 = f32[4,8,256,192,1]{2,3,4,1,0:T(8,128)} fusion(bf16[3,384,4,10,256]{4,1,0,3,2:T(8,128)(2,1)} %pad_maximum_fusion, bf16[3,3,192,384]{3,2,1,0:T(8,128)(2,1)S(1)} %copy-done.17), kind=kOutput, calls=%fused_computation.3 | convolution fusion | flops 3623878656 | bytes 25608192 | tf_op jit(solution)/shard_map/okc,kcthw->othw/dot_general | solution.py:125
  251.3 12.4 %fusion.16 = bf16[1,192,4,8,256]{4,1,3,2,0:T(8,128)(2,1)S(1)} fusion(f32[4,8,256,192,1]{2,3,4,1,0:T(8,128)} %fusion, f32[4,8,256,192,1]{2,3,4,1,0:T(8,128)} %fusion.2, f32[4,8,256]{2,1,0:T(8,128)S(1)} %copy-done.12, f32[192]{0:T(256)S(1)} %copy-done.18, bf16[3,384,4,10,256]{4,1,0,3,2:T(8,128)(2,1)} %pad_maximum_fusion, ...), kind=kOutput, calls=%fused_computation.25 | convolution fusion | flops 3631742976 | bytes 35079168 | tf_op jit(solution)/shard_map/okc,kcthw->othw/dot_general | solution.py:125
  263.8 3.5 %copy.74 = bf16[1,192,4,8,256]{4,3,2,1,0:T(8,128)(2,1)} copy(bf16[1,192,4,8,256]{4,1,3,2,0:T(8,128)(2,1)S(1)} %fusion.16) | data formatting | bytes 6291456 | tf_op jit(solution)/shard_map/broadcast_in_dim | solution.py:134
  (103 shorter events, 48.1 us)
Async XLA Ops:
  6.5 71.5 %all-gather.2.cloned.1.call-start = ((), (), s32[]{:S(2)}) async-start(), calls=%async_computation | async-start | bytes 4227072 | tf_op jit(solution)/shard_map/all_gather | solution.py:89
  14.1 74.1 %copy-start.11 = (bf16[3,3,3,384,16]{3,4,2,1,0:T(8,128)(2,1)S(1)}, bf16[3,3,3,384,16]{3,4,2,1,0:T(8,128)(2,1)}, u32[]{:S(2)}) copy-start(bf16[3,3,3,384,16]{3,4,2,1,0:T(8,128)(2,1)} %param.19) | copy-start | bytes 995332
  81.0 5.6 %collective-permute-start = (bf16[16,2,1,128]{3,0,2,1:T(8,128)(2,1)S(1)}, bf16[16,2,1,128]{3,0,2,1:T(8,128)(2,1)S(1)}, u32[]{:S(2)}, u32[]{:S(2)}) collective-permute-start(bf16[16,2,1,128]{3,0,2,1:T(8,128)(2,1)S(1)} %get-tuple-element.28), channel_id=1, source_target_pairs={{0,1},{1,2},{2,3},{3,4},{4,5},{5,6},{6,7},{8,9},{9,10},{10,11},{11... | collective-permute-start | bytes 24584 | tf_op jit(solution)/shard_map/ppermute | solution.py:17
  83.2 4.8 %collective-permute-start.1 = (bf16[16,2,1,128]{3,0,2,1:T(8,128)(2,1)S(1)}, bf16[16,2,1,128]{3,0,2,1:T(8,128)(2,1)S(1)}, u32[]{:S(2)}, u32[]{:S(2)}) collective-permute-start(bf16[16,2,1,128]{3,0,2,1:T(8,128)(2,1)S(1)} %get-tuple-element.29), channel_id=1, source_target_pairs={{1,0},{2,1},{3,2},{4,3},{5,4},{6,5},{7,6},{9,8},{10,9},{11,10},{12... | collective-permute-start | bytes 24584 | tf_op jit(solution)/shard_map/ppermute | solution.py:19
  93.1 7.6 %collective-permute-start.2 = (bf16[384,2,1,128]{0,3,2,1:T(8,128)(2,1)S(1)}, bf16[384,2,1,128]{0,3,2,1:T(8,128)(2,1)S(1)}, u32[]{:S(2)}, u32[]{:S(2)}) collective-permute-start(bf16[384,2,1,128]{0,3,2,1:T(8,128)(2,1)S(1)} %get-tuple-element.23), channel_id=1, source_target_pairs={{0,1},{1,2},{2,3},{3,4},{4,5},{5,6},{6,7},{8,9},{9,10},{10,11},{11... | collective-permute-start | bytes 589832 | tf_op jit(solution)/shard_map/ppermute | solution.py:17
  96.3 5.6 %collective-permute-start.3 = (bf16[384,2,1,128]{0,3,2,1:T(8,128)(2,1)S(1)}, bf16[384,2,1,128]{0,3,2,1:T(8,128)(2,1)S(1)}, u32[]{:S(2)}, u32[]{:S(2)}) collective-permute-start(bf16[384,2,1,128]{0,3,2,1:T(8,128)(2,1)S(1)} %get-tuple-element.24), channel_id=1, source_target_pairs={{1,0},{2,1},{3,2},{4,3},{5,4},{6,5},{7,6},{9,8},{10,9},{11,10},{12... | collective-permute-start | bytes 589832 | tf_op jit(solution)/shard_map/ppermute | solution.py:19
  115.2 3.5 %copy-start.9 = (bf16[3,384,2,4,128]{1,4,3,2,0:T(8,128)(2,1)S(1)}, bf16[3,384,2,4,128]{1,4,3,2,0:T(8,128)(2,1)}, u32[]{:S(2)}) copy-start(bf16[3,384,2,4,128]{1,4,3,2,0:T(8,128)(2,1)} %get-tuple-element.15) | copy-start | bytes 7077892
  115.2 11.9 %slice-start = ((s8[7962624]{0:T(1024)(128)(4,1)}), s8[4194304]{0:T(1024)(128)(4,1)S(1)}, s32[]{:S(2)}) async-start(s8[7962624]{0:T(1024)(128)(4,1)} %bitcast.387), calls=%async_computation.1 | async-start | bytes 8388608
  118.7 2.8 %copy-start.8 = (bf16[3,384,2,4,128]{1,4,3,2,0:T(8,128)(2,1)S(1)}, bf16[3,384,2,4,128]{1,4,3,2,0:T(8,128)(2,1)}, u32[]{:S(2)}) copy-start(bf16[3,384,2,4,128]{1,4,3,2,0:T(8,128)(2,1)} %get-tuple-element.14) | copy-start | bytes 7077892
  121.5 2.8 %copy-start.7 = (bf16[3,384,2,4,128]{1,4,3,2,0:T(8,128)(2,1)S(1)}, bf16[3,384,2,4,128]{1,4,3,2,0:T(8,128)(2,1)}, u32[]{:S(2)}) copy-start(bf16[3,384,2,4,128]{1,4,3,2,0:T(8,128)(2,1)} %get-tuple-element.13) | copy-start | bytes 7077892
  121.5 5.6 %slice-start.1 = ((s8[7962624]{0:T(1024)(128)(4,1)}), s8[3768320]{0:T(1024)(128)(4,1)S(1)}, s32[]{:S(2)}) async-start(s8[7962624]{0:T(1024)(128)(4,1)} %bitcast.387), calls=%async_computation.2 | async-start | bytes 7536640
  124.3 2.8 %copy-start.6 = (bf16[3,384,2,4,128]{1,4,3,2,0:T(8,128)(2,1)S(1)}, bf16[3,384,2,4,128]{1,4,3,2,0:T(8,128)(2,1)}, u32[]{:S(2)}) copy-start(bf16[3,384,2,4,128]{1,4,3,2,0:T(8,128)(2,1)} %get-tuple-element.12) | copy-start | bytes 7077892
  127.1 1.7 copy-start.5
  128.8 1.7 copy-start.4
  130.5 1.7 copy-start.3
  132.1 1.7 copy-start.2
  133.8 1.5 copy-start.16
  135.3 1.5 copy-start.10
  145.8 11.1 %copy-start.1 = (bf16[384,4,4,128]{3,0,2,1:T(8,128)(2,1)S(1)}, bf16[384,4,4,128]{3,0,2,1:T(8,128)(2,1)}, u32[]{:S(2)}) copy-start(bf16[384,4,4,128]{3,0,2,1:T(8,128)(2,1)} %copy-done) | copy-start | bytes 4718596
  145.8 9.6 %collective-permute-start.4 = (bf16[384,4,1,128]{3,0,2,1:T(8,128)(2,1)}, bf16[384,4,1,128]{3,0,2,1:T(8,128)(2,1)S(1)}, u32[]{:S(2)}, u32[]{:S(2)}) collective-permute-start(bf16[384,4,1,128]{3,0,2,1:T(8,128)(2,1)} %get-tuple-element.21), channel_id=1, source_target_pairs={{0,1},{1,2},{2,3},{3,4},{4,5},{5,6},{6,7},{8,9},{9,10},{10,11},{11... | collective-permute-start | bytes 1179656 | tf_op jit(solution)/shard_map/ppermute | solution.py:17
  149.3 7.6 %collective-permute-start.5 = (bf16[384,4,1,128]{3,0,2,1:T(8,128)(2,1)S(1)}, bf16[384,4,1,128]{3,0,2,1:T(8,128)(2,1)S(1)}, u32[]{:S(2)}, u32[]{:S(2)}) collective-permute-start(bf16[384,4,1,128]{3,0,2,1:T(8,128)(2,1)S(1)} %get-tuple-element.22), channel_id=1, source_target_pairs={{1,0},{2,1},{3,2},{4,3},{5,4},{6,5},{7,6},{9,8},{10,9},{11,10},{12... | collective-permute-start | bytes 1179656 | tf_op jit(solution)/shard_map/ppermute | solution.py:19
  210.7 19.9 %copy-start.17 = (bf16[3,3,192,384]{3,2,1,0:T(8,128)(2,1)S(1)}, bf16[3,3,192,384]{3,2,1,0:T(8,128)(2,1)}, u32[]{:S(2)}) copy-start(bf16[3,3,192,384]{3,2,1,0:T(8,128)(2,1)} %param.26) | copy-start | bytes 3981316
  240.9 10.4 %copy-start.12 = (f32[4,8,256]{2,1,0:T(8,128)S(1)}, f32[4,8,256]{2,1,0:T(8,128)}, u32[]{:S(2)}) copy-start(f32[4,8,256]{2,1,0:T(8,128)} %copy.73) | copy-start | bytes 98308
  241.0 10.4 %copy-start.18 = (f32[192]{0:T(256)S(1)}, f32[192]{0:T(256)}, u32[]{:S(2)}) copy-start(f32[192]{0:T(256)} %param.27) | copy-start | bytes 2308
  (4 other events, 4.0 us)
Sparse Core Ops, SparseCore 0:
  10.5 67.5 all-gather.1
where the time goes:
time: 278 us; the launch traced here: 274 us
  local copies, waits for them, and re-layouts  77.9 us (28%)
  waiting for transfers between devices  70.4 us (25%)
  matrix products  63.5 us (23%)
  other arithmetic  31.2 us (11%)
  starting transfers between devices  17.2 us (6%)
  between operations  14 us (5%)
    all_gather x1, waiting for transfers between devices, on_device(): lax.all_gather(flattened, ('req', 'tile'), axis=0, tiled=True)  64 us
    dot_general x3, matrix products, on_device(): jnp.einsum('okc,kcthw->othw', kernel, shifted[:, :, :, tap_r:tap_r + out_...  33.2 us
    another operation x2, local copies, waits for them, and re-layouts, on_device(): jnp.stack([padded[..., tap_c:tap_c + out_cols] for tap_c in range(3)], ax...  27.5 us
    dot_general x18, matrix products, causal_conv(): jnp.einsum('okc,kcthw->othw', kernel, shifted[:, :, tap_t:tap_t + frame_c...  23.3 us
    another operation x1, other arithmetic, on_device(): jnp.stack([padded[..., tap_c:tap_c + out_cols] for tap_c in range(3)], ax...  19.9 us
    reshape x1, local copies, waits for them, and re-layouts, on_device(): widened = jnp.repeat(taller, 2, axis=3)  13.1 us
    ppermute x3, starting transfers between devices, with_halo(): lax.ppermute(tail, axis, [(i, (i + 1) % count) for i in range(ends)])  8.77 us
    ppermute x3, starting transfers between devices, with_halo(): lax.ppermute(head, axis, [((i + 1) % count, i) for i in range(ends)])  8.4 us
  transfers between devices with their start and end apart: 7, of which 5 were waited for; matrix products, arithmetic and copies ran while one was open for 3% of the time, Pallas kernels for 0%

commit v1 on v0

v1 whole, which is shorter than its diff:
```python
import functools

import jax
import jax.numpy as jnp
from jax import lax
from jax.experimental import pallas as pl
from jax.experimental.pallas import tpu as pltpu
from jax.sharding import PartitionSpec as P

LAT = 16
MID = 384
OUT = 192
FRAMES = 2
ROWS = 4
COLS = 128
BF = jnp.bfloat16
F32 = jnp.float32


def taps_of(frame):
    return [(tap, frame - 2 + tap) for tap in range(3) if frame - 2 + tap >= 0]


def column(vec_ref):
    return jnp.transpose(jnp.broadcast_to(vec_ref[...], (COLS, vec_ref.shape[1])))


def shifts(x):
    col = lax.broadcasted_iota(jnp.int32, x.shape, 1)
    before = jnp.where(col == 0, 0.0, pltpu.roll(x, 1, 1))
    after = jnp.where(col == COLS - 1, 0.0, pltpu.roll(x, COLS - 1, 1))
    return before, x, after


def decode_kernel(
    info,
    rim_a,
    rim_b,
    rim_c,
    rim_d,
    b_in,
    gain,
    b_res,
    b_time,
    b_up,
    w_in_hbm,
    w_res_hbm,
    w_time_hbm,
    w_up_hbm,
    out_hbm,
    w_in,
    w_res,
    w_time,
    w_up,
    lat_cols,
    conv,
    first,
    norm_cols,
    block,
    time_cols,
    w_phase,
    bias_mid,
    bias_time,
    bias_up,
    spread,
    tall,
    out_buf,
    in_sems,
    out_sems,
):
    loads = [
        pltpu.make_async_copy(w_in_hbm, w_in, in_sems.at[0]),
        pltpu.make_async_copy(w_up_hbm, w_up, in_sems.at[1]),
        pltpu.make_async_copy(w_res_hbm.at[pl.ds(9, 18)], w_res, in_sems.at[2]),
        pltpu.make_async_copy(w_time_hbm.at[pl.ds(1, 2)], w_time, in_sems.at[3]),
    ]
    for load in loads:
        load.start()
    odd = info[0] == 1
    frame_limit, row_limit, col_limit, row_base = info[1], info[2], info[3], info[4]
    cols = lax.broadcasted_iota(jnp.int32, (1, COLS), 1)
    col_mask = (cols < col_limit).astype(F32)

    def mask_at(frame, row):
        inside = (frame < frame_limit) & (row >= 0) & (row < row_limit)
        return col_mask * jnp.where(inside, 1.0, 0.0).astype(F32)

    bias_mid[0] = column(b_in)
    bias_mid[1] = column(gain)
    bias_mid[2] = column(b_res)
    bias_time[...] = column(b_time)
    bias_up[...] = column(b_up)
    key = lax.broadcasted_iota(jnp.int32, (2 * COLS, 2 * COLS), 0)
    place = lax.broadcasted_iota(jnp.int32, (2 * COLS, 2 * COLS), 1)
    spread[...] = (key == (place % 2) * COLS + place // 2).astype(F32).astype(BF)

    for frame in range(FRAMES):
        main_even, main_odd = (rim_a, rim_b) if frame == 0 else (rim_b, rim_a)
        rest_even, rest_odd = (rim_d, rim_c) if frame == 0 else (rim_c, rim_d)
        for row in range(10):
            even = rest_even[row] if row < 3 else main_even[row - 3]
            other = main_odd[row] if row < 7 else rest_odd[row - 7]
            value = jnp.where(odd, other.astype(F32), even.astype(F32))
            value = value * mask_at(frame, row_base - 3 + row)
            for at, moved in enumerate(shifts(value)):
                lat_cols[frame, row, pl.ds(at * LAT, LAT), :] = moved.astype(BF)

    loads[0].wait()
    for frame in range(FRAMES):
        taps = taps_of(frame)
        weight = w_in[pl.ds(taps[0][0] * 9 * LAT, len(taps) * 9 * LAT), :]
        pieces = []
        for row in range(8):
            pieces.append(
                jnp.concatenate(
                    [lat_cols[src, row + d] for _, src in taps for d in range(3)], axis=0
                )
            )
        data = jnp.concatenate(pieces, axis=1)
        summed = lax.dot_general(
            weight, data, (((0,), (0,)), ((), ())), preferred_element_type=F32
        )
        for row in range(8):
            conv[frame * 8 + row] = summed[:, row * COLS : (row + 1) * COLS]

    def norm_row(at, carry):
        frame, row = at // 8, at % 8
        value = (conv[at] + bias_mid[0]).astype(BF)
        first[at] = value
        value = value.astype(F32)
        mean = jnp.sum(value * value, axis=0, keepdims=True) * (1.0 / MID)
        scaled = value * lax.rsqrt(mean + 1e-6) * bias_mid[1]
        normed = scaled / (1.0 + jnp.exp(-scaled)) * mask_at(frame, row_base - 2 + row)
        for tap, moved in enumerate(shifts(normed)):
            norm_cols[at, pl.ds(tap * MID, MID), :] = moved.astype(BF)
        return carry

    lax.fori_loop(0, FRAMES * 8, norm_row, 0)

    loads[1].wait()

    def two(phase, taps):
        return (taps[0], taps[1] + taps[2]) if phase == 0 else (taps[0] + taps[1], taps[2])

    def combine(at, carry):
        base = pl.multiple_of(at * 16, 16)
        whole = [
            [w_up[3 * d + e, pl.ds(base, 16), :].astype(F32) for e in range(3)] for d in range(3)
        ]
        for pr in range(2):
            rows = [two(pr, [whole[d][e] for d in range(3)]) for e in range(3)]
            for dr in range(2):
                for pc in range(2):
                    cells = two(pc, [rows[e][dr] for e in range(3)])
                    for dc in range(2):
                        w_phase[2 * pr + pc, pl.ds(base, 16), pl.ds((2 * dr + dc) * MID, MID)] = (
                            cells[dc].astype(BF)
                        )
        return carry

    lax.fori_loop(0, OUT // 16, combine, 0)

    loads[2].wait()

    def res_pair(pair, carry):
        for frame in range(FRAMES):
            left, right, weights = [], [], []
            for tap, src in taps_of(frame):
                for d in range(3):
                    left.append(norm_cols[src * 8 + 2 * pair + d])
                    right.append(norm_cols[src * 8 + 2 * pair + 1 + d])
                weights += [w_res[(tap - 1) * 9 + k] for k in range(9)]
            data = jnp.concatenate(
                [jnp.concatenate(left, axis=0), jnp.concatenate(right, axis=0)], axis=1
            )
            summed = jnp.dot(jnp.concatenate(weights, axis=1), data, preferred_element_type=F32)
            for k in range(2):
                value = first[frame * 8 + 2 * pair + k + 1].astype(F32) + (
                    summed[:, k * COLS : (k + 1) * COLS] + bias_mid[2]
                )
                block[frame * 6 + 2 * pair + k] = value.astype(BF)
        return carry

    lax.fori_loop(0, 3, res_pair, 0)

    loads[3].wait()

    def time_pair(pair, carry):
        for frame in range(FRAMES):
            taps = taps_of(frame)
            data = jnp.concatenate(
                [
                    jnp.concatenate([block[src * 6 + 2 * pair + k] for _, src in taps], axis=0)
                    for k in range(2)
                ],
                axis=1,
            )
            weight = jnp.concatenate([w_time[tap - 1] for tap, _ in taps], axis=1)
            summed = jnp.dot(weight, data, preferred_element_type=F32)
            for k in range(2):
                row_mask = mask_at(frame, row_base - 1 + 2 * pair + k)
                for half in range(2):
                    value = (
                        summed[half * MID : (half + 1) * MID, k * COLS : (k + 1) * COLS]
                        + bias_time[pl.ds(half * MID, MID), :]
                    ) * row_mask
                    at = (2 * frame + half) * 6 + 2 * pair + k
                    for tap, moved in enumerate(shifts(value)):
                        time_cols[at, pl.ds(tap * MID, MID), :] = moved.astype(BF)
        return carry

    lax.fori_loop(0, 3, time_pair, 0)

    def out_copy(frame, slot):
        return pltpu.make_async_copy(out_buf.at[slot], out_hbm.at[:, frame], out_sems.at[slot])

    def up_frame(frame, carry):
        slot = frame % 2

        @pl.when(frame >= 2)
        def _():
            out_copy(frame, slot).wait()

        for pair in range(2):
            for pr in range(2):
                done = []
                for pc in range(2):
                    data = jnp.concatenate(
                        [
                            jnp.concatenate(
                                [
                                    time_cols[
                                        frame * 6 + 2 * pair + k + pr + dr,
                                        pl.ds(pc * MID, 2 * MID),
                                        :,
                                    ]
                                    for dr in range(2)
                                ],
                                axis=0,
                            )
                            for k in range(2)
                        ],
                        axis=1,
                    )
                    done.append(
                        jnp.dot(w_phase[2 * pr + pc], data, preferred_element_type=F32)
                    )
                for k in range(2):
                    row_mask = mask_at(frame // 2, row_base + 2 * pair + k)
                    mixed = jnp.concatenate(
                        [
                            ((d[:, k * COLS : (k + 1) * COLS] + bias_up[...]) * row_mask).astype(BF)
                            for d in done
                        ],
                        axis=1,
                    )
                    wide = jnp.dot(mixed, spread[...], preferred_element_type=F32)
                    at = 2 * (2 * pair + k) + pr
                    for half in range(2):
                        tall[half, pl.ds(at, OUT, stride=8), :] = wide[
                            :, half * COLS : (half + 1) * COLS
                        ]
        for half in range(2):
            out_buf[slot, :, :, pl.ds(half * COLS, COLS)] = (
                tall[half].reshape(OUT, 8, COLS).astype(BF)
            )
        out_copy(frame, slot).start()
        return carry

    lax.fori_loop(0, 2 * FRAMES, up_frame, 0)
    out_copy(2, 0).wait()
    out_copy(3, 1).wait()


def decode(info, rims, vectors, weights):
    hbm = pl.BlockSpec(memory_space=pl.ANY)
    vmem = pl.BlockSpec(memory_space=pltpu.VMEM)
    return pl.pallas_call(
        decode_kernel,
        out_shape=jax.ShapeDtypeStruct((OUT, 2 * FRAMES, 2 * ROWS, 2 * COLS), BF),
        in_specs=[pl.BlockSpec(memory_space=pltpu.SMEM)] + [vmem] * 9 + [hbm] * 4,
        out_specs=hbm,
        scratch_shapes=[
            pltpu.VMEM((27 * LAT, MID), BF),
            pltpu.VMEM((18, MID, MID), BF),
            pltpu.VMEM((2, 2 * MID, MID), BF),
            pltpu.VMEM((9, OUT, MID), BF),
            pltpu.VMEM((FRAMES, 10, 3 * LAT, COLS), BF),
            pltpu.VMEM((FRAMES * 8, MID, COLS), F32),
            pltpu.VMEM((FRAMES * 8, MID, COLS), BF),
            pltpu.VMEM((FRAMES * 8, 3 * MID, COLS), BF),
            pltpu.VMEM((FRAMES * 6, MID, COLS), BF),
            pltpu.VMEM((2 * FRAMES * 6, 3 * MID, COLS), BF),
            pltpu.VMEM((4, OUT, 4 * MID), BF),
            pltpu.VMEM((3, MID, COLS), F32),
            pltpu.VMEM((2 * MID, COLS), F32),
            pltpu.VMEM((OUT, COLS), F32),
            pltpu.VMEM((2 * COLS, 2 * COLS), BF),
            pltpu.VMEM((2, OUT * 8, COLS), F32),
            pltpu.VMEM((2, OUT, 8, 2 * COLS), BF),
            pltpu.SemaphoreType.DMA((4,)),
            pltpu.SemaphoreType.DMA((2,)),
        ],
        compiler_params=pltpu.CompilerParams(vmem_limit_bytes=44 << 20),
        cost_estimate=pl.CostEstimate(
            flops=13_000_000_000, bytes_accessed=13_000_000, transcendentals=800_000
        ),
    )(info, *rims, *vectors, *weights)


def pick(options, chosen):
    result = options[0]
    for k in range(1, len(options)):
        result = jnp.where(chosen == k, options[k], result)
    return result


def on_device(
    latents,
    piece_dest,
    frames,
    heights,
    widths,
    w_in,
    b_in,
    gain_norm,
    w_res,
    b_res,
    w_time,
    b_time,
    w_up,
    b_up,
):
    group, tile = lax.axis_index("req"), lax.axis_index("tile")
    ring = 4
    along_x, along_z = group // ring, group % ring

    def shift_x(value, k):
        return lax.ppermute(
            value,
            "req",
            [(x * ring + z, (x + k) % ring * ring + z) for x in range(ring) for z in range(ring)],
        )

    def shift_z(value, k):
        return lax.ppermute(
            value,
            "req",
            [(x * ring + z, x * ring + (z + k) % ring) for x in range(ring) for z in range(ring)],
        )

    wanted = piece_dest.reshape(ring * ring, -1)[:, 0] // (FRAMES * 32)
    held = [latents] + [shift_x(latents, k) for k in range(1, ring)]
    held_for = [wanted[(along_x - k) % ring * ring + along_z] for k in range(ring)]

    def select_for(target):
        chosen = jnp.int32(0)
        for k in range(1, ring):
            chosen = jnp.where(held_for[k] == target, k, chosen)
        return pick(held, chosen)

    arrived = [select_for(group)]
    for k in range(1, ring):
        arrived.append(shift_z(select_for(along_x * ring + (along_z + k) % ring), k))
    source = jnp.argmax(wanted == group).astype(jnp.int32)
    mine = pick(arrived, (along_z - source % ring) % ring)

    late = tile >= 4
    upper, lower = mine[0:7], mine[1:8]
    head, tail = mine[0:3], mine[5:8]
    quarter = range(4)
    rims = [
        lax.ppermute(
            jnp.where(late, lower, upper),
            "tile",
            [(s, 2 * s) for s in quarter] + [(4 + s, 2 * s + 1) for s in quarter],
        ),
        lax.ppermute(
            jnp.where(late, upper, lower),
            "tile",
            [(s, 2 * s + 1) for s in quarter] + [(4 + s, 2 * s) for s in quarter],
        ),
        lax.ppermute(
            jnp.where(late, tail, head),
            "tile",
            [(s, 2 * s - 1) for s in quarter if s > 0]
            + [(4 + s, 2 * s + 2) for s in quarter if s < 3],
        ),
        lax.ppermute(
            jnp.where(late, head, tail),
            "tile",
            [(s, 2 * s + 2) for s in quarter if s < 3]
            + [(4 + s, 2 * s - 1) for s in quarter if s > 0],
        ),
    ]
    info = jnp.stack(
        [tile % 2, frames[group], heights[group], widths[group], tile * ROWS]
    ).astype(jnp.int32)
    vectors = [v.reshape(1, -1) for v in (b_in, gain_norm, b_res, b_time, b_up)]
    weights = [
        jnp.swapaxes(w_in, 3, 4).reshape(27 * LAT, MID),
        w_res.reshape(27, MID, MID),
        w_time,
        w_up.reshape(9, OUT, MID),
    ]
    return decode(info, rims, vectors, weights)[None]


def solution(mesh):
    return jax.shard_map(
        on_device,
        mesh=mesh,
        in_specs=(P(("req", "tile"), None, None),) + (P(),) * 13,
        out_specs=P("req", None, None, "tile", None),
        check_vma=False,
    )
```

time: 278 us -> 74.9 us (0.27)
  waiting for transfers between devices: 70.4 us -> 0.03 us
  local copies, waits for them, and re-layouts: 77.9 us -> 14.4 us
  matrix products: 63.5 us -> 0 us
  other arithmetic: 31.2 us -> 2.33 us
  Pallas kernels: 0 us -> 25.9 us
  between operations: 14 us -> 9.75 us
  starting transfers between devices: 17.2 us -> 21.2 us
    all_gather x1 -> x0, waiting for transfers between devices: 64 us -> none  [on_device(): lax.all_gather(flattened, ('req', 'tile'), axis=0, tiled=True)]
    dot_general x25 -> x0, matrix products: 63.5 us -> none  [the longest x3 33.2 us: on_device(): jnp.einsum('okc,kcthw->othw', kernel, shifted[:, :, :, tap_r:tap_r + out_...]
    another operation x6 -> x1, local copies, waits for them, and re-layouts: 32 us -> 1.95 us  [on_device(): jnp.stack([tile % 2, frames[group], heights[group], widths[group], tile *...]
    pallas_call x0 -> x1, Pallas kernels: none -> 25.9 us  [decode(): pl.pallas_call(decode_kernel, out_shape=jax.ShapeDtypeStruct((OUT, 2 * FR...]
    another operation x3 -> x1, other arithmetic: 22.8 us -> 0.74 us  [on_device(): source = jnp.argmax(wanted == group).astype(jnp.int32)]
    slice x6 -> x1, local copies, waits for them, and re-layouts: 10.8 us -> 0.12 us  [on_device(): wanted = piece_dest.reshape(ring * ring, -1)[:, 0] // (FRAMES * 32)]
    reshape x2 -> x5, local copies, waits for them, and re-layouts: 13.2 us -> 3.49 us  [the longest x4 2.74 us: on_device(): vectors = [v.reshape(1, -1) for v in (b_in, gain_norm, b_res, b_time, b_up)]]
    broadcast_in_dim x6 -> x0, local copies, waits for them, and re-layouts: 9.62 us -> none  [the longest x1 4.13 us: on_device(): widened = jnp.repeat(taller, 2, axis=3)]
  transfers between devices with their start and end apart: 7 -> 10, of which waited for: 5 -> 0; matrix products, arithmetic and copies ran while one was open for 3% -> 15% of each run, Pallas kernels for 0% -> 0%
where the time goes in v1:
time: 74.9 us; the launch traced here: 73.7 us
  Pallas kernels  25.9 us (35%)
  starting transfers between devices  21.2 us (28%)
  local copies, waits for them, and re-layouts  14.4 us (19%)
  between operations  9.75 us (13%)
  other arithmetic  2.33 us (3%)
    pallas_call x1, Pallas kernels, decode(): pl.pallas_call(decode_kernel, out_shape=jax.ShapeDtypeStruct((OUT, 2 * FR...  25.9 us
    ppermute x3, starting transfers between devices, shift_z(): lax.ppermute(value, 'req', [(x * ring + z, x * ring + (z + k) % ring) for...  6.58 us
    ppermute x3, starting transfers between devices, shift_x(): lax.ppermute(value, 'req', [(x * ring + z, (x + k) % ring * ring + z) for...  5.65 us
    unnamed x8, local copies, waits for them, and re-layouts  4.45 us
    ppermute x1, starting transfers between devices, on_device(): lax.ppermute(jnp.where(late, lower, upper), 'tile', [(s, 2 * s) for s in...  3.8 us
    ppermute x1, starting transfers between devices, on_device(): lax.ppermute(jnp.where(late, head, tail), 'tile', [(s, 2 * s + 2) for s i...  3.2 us
    reshape x4, local copies, waits for them, and re-layouts, on_device(): vectors = [v.reshape(1, -1) for v in (b_in, gain_norm, b_res, b_time, b_up)]  2.74 us
    another operation x1, local copies, waits for them, and re-layouts, on_device(): jnp.stack([tile % 2, frames[group], heights[group], widths[group], tile *...  1.95 us
  transfers between devices with their start and end apart: 10, of which 0 were waited for; matrix products, arithmetic and copies ran while one was open for 15% of the time, Pallas kernels for 0%

profile of v1, /device:TPU:8, one launch (start us, length us, event | category | flops | bytes accessed | tf_op | source)
XLA Modules:
  0.0 73.7 jit_solution(5512856520211936925)
XLA Ops:
  0.0 1.5 %collective-permute-start.2 = (bf16[8,16,128]{2,1,0:T(8,128)(2,1)}, bf16[8,16,128]{2,1,0:T(8,128)(2,1)S(1)}, u32[]{:S(2)}, u32[]{:S(2)}) collective-permute-start(bf16[8,16,128]{2,1,0:T(8,128)(2,1)} %param.14), channel_id=1, source_target_pairs={{0,32},{8,40},{16,48},{24,56},{32,64},{40,72},{48,80},{56,88},{64,... | collective-permute-start | bytes 98312 | tf_op jit(solution)/shard_map/ppermute | solution.py:339
  1.5 2.7 %collective-permute-start.1 = (bf16[8,16,128]{2,1,0:T(8,128)(2,1)}, bf16[8,16,128]{2,1,0:T(8,128)(2,1)S(1)}, u32[]{:S(2)}, u32[]{:S(2)}) collective-permute-start(bf16[8,16,128]{2,1,0:T(8,128)(2,1)} %param.14), channel_id=1, source_target_pairs={{0,64},{8,72},{16,80},{24,88},{32,96},{40,104},{48,112},{56,120},{... | collective-permute-start | bytes 98312 | tf_op jit(solution)/shard_map/ppermute | solution.py:339
  4.2 1.4 %collective-permute-start = (bf16[8,16,128]{2,1,0:T(8,128)(2,1)}, bf16[8,16,128]{2,1,0:T(8,128)(2,1)S(1)}, u32[]{:S(2)}, u32[]{:S(2)}) collective-permute-start(bf16[8,16,128]{2,1,0:T(8,128)(2,1)} %param.14), channel_id=1, source_target_pairs={{0,96},{8,104},{16,112},{24,120},{32,0},{40,8},{48,16},{56,24},{64... | collective-permute-start | bytes 98312 | tf_op jit(solution)/shard_map/ppermute | solution.py:339
  5.7 0.8 %reshape.27 = s32[16,64]{1,0:T(8,128)S(1)} reshape(s32[1024]{0:T(1024)} %param.15) | data formatting | bytes 8192 | tf_op jit(solution)/shard_map/reshape | solution.py:352
  12.8 0.8 %select_select_fusion.1 = (bf16[8,16,128]{2,1,0:T(8,128)(2,1)S(1)}, bf16[8,16,128]{2,1,0:T(8,128)(2,1)S(1)}, bf16[8,16,128]{2,1,0:T(8,128)(2,1)S(1)}) fusion(bf16[8,16,128]{2,1,0:T(8,128)(2,1)S(1)} %collective-permute-done, bf16[8,16,128]{2,1,0:T(8,128)(2,1)S(1)} %collective-permute-done.1, bf16[8,16,128]{2,1,0:T(8,128)(2,1)S(1)} %collective-permute-done.2, ...), kind=kLoop, calls=%fused_computation.1 | loop fusion | flops 147456 | bytes 229385 | tf_op jit(solution)/shard_map/jit(_where)/select_n | solution.py:314
  13.6 2.0 %collective-permute-start.5 = (bf16[8,16,128]{2,1,0:T(8,128)(2,1)S(1)}, bf16[8,16,128]{2,1,0:T(8,128)(2,1)S(1)}, u32[]{:S(2)}, u32[]{:S(2)}) collective-permute-start(bf16[8,16,128]{2,1,0:T(8,128)(2,1)S(1)} %get-tuple-element.7), channel_id=1, source_target_pairs={{0,8},{8,16},{16,24},{24,0},{32,40},{40,48},{48,56},{56,32},{64,72... | collective-permute-start | bytes 98312 | tf_op jit(solution)/shard_map/ppermute | solution.py:346
  15.6 3.6 %collective-permute-start.4 = (bf16[8,16,128]{2,1,0:T(8,128)(2,1)S(1)}, bf16[8,16,128]{2,1,0:T(8,128)(2,1)S(1)}, u32[]{:S(2)}, u32[]{:S(2)}) collective-permute-start(bf16[8,16,128]{2,1,0:T(8,128)(2,1)S(1)} %get-tuple-element.8), channel_id=1, source_target_pairs={{0,16},{8,24},{16,0},{24,8},{32,48},{40,56},{48,32},{56,40},{64,80... | collective-permute-start | bytes 98312 | tf_op jit(solution)/shard_map/ppermute | solution.py:346
  19.2 1.0 %collective-permute-start.3 = (bf16[8,16,128]{2,1,0:T(8,128)(2,1)S(1)}, bf16[8,16,128]{2,1,0:T(8,128)(2,1)S(1)}, u32[]{:S(2)}, u32[]{:S(2)}) collective-permute-start(bf16[8,16,128]{2,1,0:T(8,128)(2,1)S(1)} %get-tuple-element.9), channel_id=1, source_target_pairs={{0,24},{8,0},{16,8},{24,16},{32,56},{40,32},{48,40},{56,48},{64,88... | collective-permute-start | bytes 98312 | tf_op jit(solution)/shard_map/ppermute | solution.py:346
  20.2 0.7 compare_reduce_fusion
  24.9 0.8 %select_select_fusion = bf16[8,16,128]{2,1,0:T(8,128)(2,1)S(1)} fusion(bf16[8,16,128]{2,1,0:T(8,128)(2,1)S(1)} %collective-permute-done.3, bf16[8,16,128]{2,1,0:T(8,128)(2,1)S(1)} %collective-permute-done.4, bf16[8,16,128]{2,1,0:T(8,128)(2,1)S(1)} %collective-permute-done.5, bf16[8,16,128]{2,1,0:T(8,128)(2,1)S(1)} %collective-permute-done, ...), kind=kLoop, calls=%fused_computation | loop fusion | flops 98304 | bytes 262150 | tf_op jit(solution)/shard_map/jit(_where)/select_n | solution.py:314
  25.8 3.8 %collective-permute-start.6 = (bf16[7,16,128]{2,1,0:T(8,128)(2,1)S(1)}, bf16[7,16,128]{2,1,0:T(8,128)(2,1)S(1)}, u32[]{:S(2)}, u32[]{:S(2)}) collective-permute-start(bf16[7,16,128]{2,1,0:T(8,128)(2,1)S(1)} %get-tuple-element.13), channel_id=1, source_target_pairs={{0,0},{1,2},{2,4},{3,6},{4,1},{5,3},{6,5},{7,7},{8,8},{9,10},{10,1... | collective-permute-start | bytes 86024 | tf_op jit(solution)/shard_map/ppermute | solution.py:373
  29.6 3.2 %collective-permute-start.9 = (bf16[3,16,128]{2,1,0:T(8,128)(2,1)S(1)}, bf16[3,16,128]{2,1,0:T(8,128)(2,1)S(1)}, u32[]{:S(2)}, u32[]{:S(2)}) collective-permute-start(bf16[3,16,128]{2,1,0:T(8,128)(2,1)S(1)} %get-tuple-element.10), channel_id=1, source_target_pairs={{0,2},{1,4},{2,6},{5,1},{6,3},{7,5},{8,10},{9,12},{10,14},{13,9},{... | collective-permute-start | bytes 36872 | tf_op jit(solution)/shard_map/ppermute | solution.py:389
  32.8 1.9 %collective-permute-start.8 = (bf16[3,16,128]{2,1,0:T(8,128)(2,1)S(1)}, bf16[3,16,128]{2,1,0:T(8,128)(2,1)S(1)}, u32[]{:S(2)}, u32[]{:S(2)}) collective-permute-start(bf16[3,16,128]{2,1,0:T(8,128)(2,1)S(1)} %get-tuple-element.11), channel_id=1, source_target_pairs={{1,1},{2,3},{3,5},{4,2},{5,4},{6,6},{9,9},{10,11},{11,13},{12,10},... | collective-permute-start | bytes 36872 | tf_op jit(solution)/shard_map/ppermute | solution.py:383
  34.8 1.3 %dynamic_slice.20 = s32[1]{0:T(128)} dynamic-slice(s32[16]{0:T(128)} %param.18, s32[]{:T(128)S(6)} %select_n.224), dynamic_slice_sizes={1} | dynamic-slice | bytes 12 | tf_op jit(solution)/shard_map/dynamic_slice | solution.py:397
  36.1 1.2 %dynamic_slice.19 = s32[1]{0:T(128)} dynamic-slice(s32[16]{0:T(128)} %param.17, s32[]{:T(128)S(6)} %select_n.224), dynamic_slice_sizes={1} | dynamic-slice | bytes 12 | tf_op jit(solution)/shard_map/dynamic_slice | solution.py:397
  37.3 1.2 %dynamic_slice.18 = s32[1]{0:T(128)} dynamic-slice(s32[16]{0:T(128)} %param.16, s32[]{:T(128)S(6)} %select_n.224), dynamic_slice_sizes={1} | dynamic-slice | bytes 12 | tf_op jit(solution)/shard_map/dynamic_slice | solution.py:397
  38.6 0.7 reshape.28.b_in
  39.2 0.7 reshape.29.gain
  40.6 0.7 reshape.31.b_time
  41.3 1.9 %stack.11.info = s32[5]{0:T(128)S(1)} concatenate(s32[1]{0:T(128)} %bitcast, s32[1]{0:T(128)} %dynamic_slice.18, s32[1]{0:T(128)} %dynamic_slice.19, s32[1]{0:T(128)} %dynamic_slice.20, s32[1]{0:T(128)} %bitcast.1), dimensions={0} | concatenate | bytes 40 | tf_op jit(solution)/shard_map/stack | solution.py:396
  43.3 1.5 %copy-done = bf16[3,768,384]{2,1,0:T(8,128)(2,1)S(1)} copy-done((bf16[3,768,384]{2,1,0:T(8,128)(2,1)S(1)}, bf16[3,768,384]{2,1,0:T(8,128)(2,1)}, u32[]{:S(2)}) %copy-start) | copy-done | bytes 1769496
  44.8 1.3 %copy-done.1 = bf16[3,3,192,384]{3,2,1,0:T(8,128)(2,1)S(1)} copy-done((bf16[3,3,192,384]{3,2,1,0:T(8,128)(2,1)S(1)}, bf16[3,3,192,384]{3,2,1,0:T(8,128)(2,1)}, u32[]{:S(2)}) %copy-start.1) | copy-done | bytes 1327128
  46.1 1.0 %copy-done.2 = bf16[3,3,3,384,16]{3,4,2,1,0:T(8,128)(2,1)S(1)} copy-done((bf16[3,3,3,384,16]{3,4,2,1,0:T(8,128)(2,1)S(1)}, bf16[3,3,3,384,16]{3,4,2,1,0:T(8,128)(2,1)}, u32[]{:S(2)}) %copy-start.2) | copy-done | bytes 331800
  47.7 25.9 %shard_map.136 = bf16[192,4,8,256]{3,2,1,0:T(8,128)(2,1)} custom-call(s32[5]{0:T(128)S(1)} %stack.11.info, bf16[7,16,128]{2,1,0:T(8,128)(2,1)S(1)} %collective-permute-done.6.rim_a, bf16[7,16,128]{2,1,0:T(8,128)(2,1)S(1)} %collective-permute-done.7.rim_b, bf16[3,16,128]{2,1,0:T(8,128)(2,1)S(1)} %collective-permute-done.8.rim_c, ...), custom_call_target="tpu_custom_call" | custom-call | flops 12999999488 | bytes 13000000 | tf_op jit(solution)/shard_map/pallas_call | solution.py:278
  (22 shorter events, 2.2 us)
Async XLA Ops:
  0.0 12.8 %collective-permute-start.2 = (bf16[8,16,128]{2,1,0:T(8,128)(2,1)}, bf16[8,16,128]{2,1,0:T(8,128)(2,1)S(1)}, u32[]{:S(2)}, u32[]{:S(2)}) collective-permute-start(bf16[8,16,128]{2,1,0:T(8,128)(2,1)} %param.14), channel_id=1, source_target_pairs={{0,32},{8,40},{16,48},{24,56},{32,64},{40,72},{48,80},{56,88},{64,... | collective-permute-start | bytes 98312 | tf_op jit(solution)/shard_map/ppermute | solution.py:339
  1.5 11.3 %collective-permute-start.1 = (bf16[8,16,128]{2,1,0:T(8,128)(2,1)}, bf16[8,16,128]{2,1,0:T(8,128)(2,1)S(1)}, u32[]{:S(2)}, u32[]{:S(2)}) collective-permute-start(bf16[8,16,128]{2,1,0:T(8,128)(2,1)} %param.14), channel_id=1, source_target_pairs={{0,64},{8,72},{16,80},{24,88},{32,96},{40,104},{48,112},{56,120},{... | collective-permute-start | bytes 98312 | tf_op jit(solution)/shard_map/ppermute | solution.py:339
  4.2 8.6 %collective-permute-start = (bf16[8,16,128]{2,1,0:T(8,128)(2,1)}, bf16[8,16,128]{2,1,0:T(8,128)(2,1)S(1)}, u32[]{:S(2)}, u32[]{:S(2)}) collective-permute-start(bf16[8,16,128]{2,1,0:T(8,128)(2,1)} %param.14), channel_id=1, source_target_pairs={{0,96},{8,104},{16,112},{24,120},{32,0},{40,8},{48,16},{56,24},{64... | collective-permute-start | bytes 98312 | tf_op jit(solution)/shard_map/ppermute | solution.py:339
  13.6 11.3 %collective-permute-start.5 = (bf16[8,16,128]{2,1,0:T(8,128)(2,1)S(1)}, bf16[8,16,128]{2,1,0:T(8,128)(2,1)S(1)}, u32[]{:S(2)}, u32[]{:S(2)}) collective-permute-start(bf16[8,16,128]{2,1,0:T(8,128)(2,1)S(1)} %get-tuple-element.7), channel_id=1, source_target_pairs={{0,8},{8,16},{16,24},{24,0},{32,40},{40,48},{48,56},{56,32},{64,72... | collective-permute-start | bytes 98312 | tf_op jit(solution)/shard_map/ppermute | solution.py:346
  15.6 9.3 %collective-permute-start.4 = (bf16[8,16,128]{2,1,0:T(8,128)(2,1)S(1)}, bf16[8,16,128]{2,1,0:T(8,128)(2,1)S(1)}, u32[]{:S(2)}, u32[]{:S(2)}) collective-permute-start(bf16[8,16,128]{2,1,0:T(8,128)(2,1)S(1)} %get-tuple-element.8), channel_id=1, source_target_pairs={{0,16},{8,24},{16,0},{24,8},{32,48},{40,56},{48,32},{56,40},{64,80... | collective-permute-start | bytes 98312 | tf_op jit(solution)/shard_map/ppermute | solution.py:346
  19.2 5.7 %collective-permute-start.3 = (bf16[8,16,128]{2,1,0:T(8,128)(2,1)S(1)}, bf16[8,16,128]{2,1,0:T(8,128)(2,1)S(1)}, u32[]{:S(2)}, u32[]{:S(2)}) collective-permute-start(bf16[8,16,128]{2,1,0:T(8,128)(2,1)S(1)} %get-tuple-element.9), channel_id=1, source_target_pairs={{0,24},{8,0},{16,8},{24,16},{32,56},{40,32},{48,40},{56,48},{64,88... | collective-permute-start | bytes 98312 | tf_op jit(solution)/shard_map/ppermute | solution.py:346
  25.7 17.5 %collective-permute-start.7 = (bf16[7,16,128]{2,1,0:T(8,128)(2,1)S(1)}, bf16[7,16,128]{2,1,0:T(8,128)(2,1)S(1)}, u32[]{:S(2)}, u32[]{:S(2)}) collective-permute-start(bf16[7,16,128]{2,1,0:T(8,128)(2,1)S(1)} %get-tuple-element.12), channel_id=1, source_target_pairs={{0,1},{1,3},{2,5},{3,7},{4,0},{5,2},{6,4},{7,6},{8,9},{9,11},{10,1... | collective-permute-start | bytes 86024 | tf_op jit(solution)/shard_map/ppermute | solution.py:378
  25.8 17.5 %collective-permute-start.6 = (bf16[7,16,128]{2,1,0:T(8,128)(2,1)S(1)}, bf16[7,16,128]{2,1,0:T(8,128)(2,1)S(1)}, u32[]{:S(2)}, u32[]{:S(2)}) collective-permute-start(bf16[7,16,128]{2,1,0:T(8,128)(2,1)S(1)} %get-tuple-element.13), channel_id=1, source_target_pairs={{0,0},{1,2},{2,4},{3,6},{4,1},{5,3},{6,5},{7,7},{8,8},{9,10},{10,1... | collective-permute-start | bytes 86024 | tf_op jit(solution)/shard_map/ppermute | solution.py:373
  29.6 13.6 %collective-permute-start.9 = (bf16[3,16,128]{2,1,0:T(8,128)(2,1)S(1)}, bf16[3,16,128]{2,1,0:T(8,128)(2,1)S(1)}, u32[]{:S(2)}, u32[]{:S(2)}) collective-permute-start(bf16[3,16,128]{2,1,0:T(8,128)(2,1)S(1)} %get-tuple-element.10), channel_id=1, source_target_pairs={{0,2},{1,4},{2,6},{5,1},{6,3},{7,5},{8,10},{9,12},{10,14},{13,9},{... | collective-permute-start | bytes 36872 | tf_op jit(solution)/shard_map/ppermute | solution.py:389
  32.8 10.4 %collective-permute-start.8 = (bf16[3,16,128]{2,1,0:T(8,128)(2,1)S(1)}, bf16[3,16,128]{2,1,0:T(8,128)(2,1)S(1)}, u32[]{:S(2)}, u32[]{:S(2)}) collective-permute-start(bf16[3,16,128]{2,1,0:T(8,128)(2,1)S(1)} %get-tuple-element.11), channel_id=1, source_target_pairs={{1,1},{2,3},{3,5},{4,2},{5,4},{6,6},{9,9},{10,11},{11,13},{12,10},... | collective-permute-start | bytes 36872 | tf_op jit(solution)/shard_map/ppermute | solution.py:383
  43.3 1.5 %copy-start = (bf16[3,768,384]{2,1,0:T(8,128)(2,1)S(1)}, bf16[3,768,384]{2,1,0:T(8,128)(2,1)}, u32[]{:S(2)}) copy-start(bf16[3,768,384]{2,1,0:T(8,128)(2,1)} %w_time_hbm.1) | copy-start | bytes 5308420
  44.8 1.3 %copy-start.1 = (bf16[3,3,192,384]{3,2,1,0:T(8,128)(2,1)S(1)}, bf16[3,3,192,384]{3,2,1,0:T(8,128)(2,1)}, u32[]{:S(2)}) copy-start(bf16[3,3,192,384]{3,2,1,0:T(8,128)(2,1)} %param.26) | copy-start | bytes 3981316
  46.1 1.0 %copy-start.2 = (bf16[3,3,3,384,16]{3,4,2,1,0:T(8,128)(2,1)S(1)}, bf16[3,3,3,384,16]{3,4,2,1,0:T(8,128)(2,1)}, u32[]{:S(2)}) copy-start(bf16[3,3,3,384,16]{3,4,2,1,0:T(8,128)(2,1)} %param.19) | copy-start | bytes 995332
  47.1 0.7 copy-start.3

commit v2 on v1

--- a/solution.py
+++ b/solution.py
@@ -22,7 +22,7 @@
 
 
 def column(vec_ref):
-    return jnp.transpose(jnp.broadcast_to(vec_ref[...], (COLS, vec_ref.shape[1])))
+    return jnp.transpose(jnp.broadcast_to(vec_ref[...][None, :], (COLS, vec_ref.shape[0])))
 
 
 def shifts(x):
@@ -32,36 +32,123 @@
     return before, x, after
 
 
+RING = 4
+PICK_Z, PICK_MINE, LATE, ODD, REGION, N_MASK = 0, 16, 20, 21, 22, 48
+
+
+def mask_kernel(piece_dest, frames, heights, widths, masks):
+    group, tile = lax.axis_index("req"), lax.axis_index("tile")
+    along_x, along_z = lax.div(group, RING), lax.rem(group, RING)
+    per_group = piece_dest.shape[0] // (RING * RING)
+
+    def wanted(p):
+        return lax.div(piece_dest[p * per_group], per_group)
+
+    def put(row, flag):
+        value = jnp.where(flag, 1.0, 0.0).astype(F32)
+        masks[pl.ds(row, 1), :] = jnp.full((1, COLS), value, F32)
+
+    held_for = [wanted(lax.rem(along_x - k + RING, RING) * RING + along_z) for k in range(RING)]
+    for j in range(RING):
+        target = along_x * RING + lax.rem(along_z + j, RING)
+        for k in range(RING):
+            put(PICK_Z + RING * j + k, held_for[k] == target)
+    source_z = jnp.int32(0)
+    for p in range(RING * RING):
+        source_z = jnp.where(wanted(p) == group, p % RING, source_z)
+    offset = lax.rem(along_z - source_z + RING, RING)
+    for j in range(RING):
+        put(PICK_MINE + j, offset == j)
+    put(LATE, tile >= 4)
+    put(ODD, lax.rem(tile, 2) == 1)
+    cols = lax.broadcasted_iota(jnp.int32, (1, COLS), 1)
+    inside_cols = (cols < widths[group]).astype(F32)
+    for frame in range(FRAMES):
+        for row in range(10):
+            at = tile * ROWS - 3 + row
+            inside = (frame < frames[group]) & (at >= 0) & (at < heights[group])
+            value = inside_cols * jnp.where(inside, 1.0, 0.0).astype(F32)
+            masks[pl.ds(REGION + 10 * frame + row, 1), :] = value
+    masks[pl.ds(REGION + 20, N_MASK - REGION - 20), :] = jnp.zeros((N_MASK - REGION - 20, COLS), F32)
+
+
+def make_masks(piece_dest, frames, heights, widths):
+    return pl.pallas_call(
+        mask_kernel,
+        out_shape=jax.ShapeDtypeStruct((N_MASK, COLS), F32),
+        in_specs=[pl.BlockSpec(memory_space=pltpu.SMEM)] * 4,
+        out_specs=pl.BlockSpec(memory_space=pltpu.VMEM),
+        cost_estimate=pl.CostEstimate(flops=100_000, bytes_accessed=30_000, transcendentals=0),
+    )(piece_dest, frames, heights, widths)
+
+
+def prepare_kernel(b_in, gain, b_res, b_time, b_up, w_up, w_phase, bias):
+    for at, vec in enumerate((b_in, gain, b_res)):
+        bias[pl.ds(at * MID, MID), :] = column(vec)
+    bias[pl.ds(3 * MID, 2 * MID), :] = column(b_time)
+    bias[pl.ds(5 * MID, OUT), :] = column(b_up)
+
+    def two(phase, taps):
+        return (taps[0], taps[1] + taps[2]) if phase == 0 else (taps[0] + taps[1], taps[2])
+
+    def combine(at, carry):
+        base = pl.multiple_of(at * 16, 16)
+        whole = [
+            [w_up[3 * d + e, pl.ds(base, 16), :].astype(F32) for e in range(3)] for d in range(3)
+        ]
+        for pr in range(2):
+            rows = [two(pr, [whole[d][e] for d in range(3)]) for e in range(3)]
+            for dr in range(2):
+                for pc in range(2):
+                    cells = two(pc, [rows[e][dr] for e in range(3)])
+                    for dc in range(2):
+                        w_phase[2 * pr + pc, pl.ds(base, 16), pl.ds((2 * dr + dc) * MID, MID)] = (
+                            cells[dc].astype(BF)
+                        )
+        return carry
+
+    lax.fori_loop(0, OUT // 16, combine, 0)
+
+
+def prepare(vectors, w_up):
+    vmem = pl.BlockSpec(memory_space=pltpu.VMEM)
+    return pl.pallas_call(
+        prepare_kernel,
+        out_shape=(
+            jax.ShapeDtypeStruct((4, OUT, 4 * MID), BF),
+            jax.ShapeDtypeStruct((5 * MID + OUT, COLS), F32),
+        ),
+        in_specs=[vmem] * 6,
+        out_specs=(vmem, vmem),
+        cost_estimate=pl.CostEstimate(
+            flops=10_000_000, bytes_accessed=5_000_000, transcendentals=0
+        ),
+    )(*vectors, w_up)
+
+
 def decode_kernel(
-    info,
+    masks,
     rim_a,
     rim_b,
     rim_c,
     rim_d,
-    b_in,
-    gain,
-    b_res,
-    b_time,
-    b_up,
+    bias_hbm,
     w_in_hbm,
     w_res_hbm,
     w_time_hbm,
-    w_up_hbm,
+    w_phase_hbm,
     out_hbm,
     w_in,
     w_res,
     w_time,
-    w_up,
+    w_phase,
+    bias,
     lat_cols,
     conv,
     first,
     norm_cols,
     block,
     time_cols,
-    w_phase,
-    bias_mid,
-    bias_time,
-    bias_up,
     spread,
     tall,
     out_buf,
@@ -70,29 +157,24 @@
 ):
     loads = [
         pltpu.make_async_copy(w_in_hbm, w_in, in_sems.at[0]),
-        pltpu.make_async_copy(w_up_hbm, w_up, in_sems.at[1]),
+        pltpu.make_async_copy(bias_hbm, bias, in_sems.at[1]),
         pltpu.make_async_copy(w_res_hbm.at[pl.ds(9, 18)], w_res, in_sems.at[2]),
         pltpu.make_async_copy(w_time_hbm.at[pl.ds(1, 2)], w_time, in_sems.at[3]),
+        pltpu.make_async_copy(w_phase_hbm, w_phase, in_sems.at[4]),
     ]
     for load in loads:
         load.start()
-    odd = info[0] == 1
-    frame_limit, row_limit, col_limit, row_base = info[1], info[2], info[3], info[4]
-    cols = lax.broadcasted_iota(jnp.int32, (1, COLS), 1)
-    col_mask = (cols < col_limit).astype(F32)
+
+    def bias_of(at, count):
+        return bias[pl.ds(at, count), :]
 
     def mask_at(frame, row):
-        inside = (frame < frame_limit) & (row >= 0) & (row < row_limit)
-        return col_mask * jnp.where(inside, 1.0, 0.0).astype(F32)
-
-    bias_mid[0] = column(b_in)
-    bias_mid[1] = column(gain)
-    bias_mid[2] = column(b_res)
-    bias_time[...] = column(b_time)
-    bias_up[...] = column(b_up)
+        return masks[pl.ds(REGION + 10 * frame + row, 1), :]
+
     key = lax.broadcasted_iota(jnp.int32, (2 * COLS, 2 * COLS), 0)
     place = lax.broadcasted_iota(jnp.int32, (2 * COLS, 2 * COLS), 1)
     spread[...] = (key == (place % 2) * COLS + place // 2).astype(F32).astype(BF)
+    odd = jnp.broadcast_to(masks[pl.ds(ODD, 1), :], (LAT, COLS)) > 0.5
 
     for frame in range(FRAMES):
         main_even, main_odd = (rim_a, rim_b) if frame == 0 else (rim_b, rim_a)
@@ -101,7 +183,7 @@
             even = rest_even[row] if row < 3 else main_even[row - 3]
             other = main_odd[row] if row < 7 else rest_odd[row - 7]
             value = jnp.where(odd, other.astype(F32), even.astype(F32))
-            value = value * mask_at(frame, row_base - 3 + row)
+            value = value * mask_at(frame, row)
             for at, moved in enumerate(shifts(value)):
                 lat_cols[frame, row, pl.ds(at * LAT, LAT), :] = moved.astype(BF)
 
@@ -123,42 +205,21 @@
         for row in range(8):
             conv[frame * 8 + row] = summed[:, row * COLS : (row + 1) * COLS]
 
+    loads[1].wait()
+
     def norm_row(at, carry):
         frame, row = at // 8, at % 8
-        value = (conv[at] + bias_mid[0]).astype(BF)
+        value = (conv[at] + bias_of(0, MID)).astype(BF)
         first[at] = value
         value = value.astype(F32)
         mean = jnp.sum(value * value, axis=0, keepdims=True) * (1.0 / MID)
-        scaled = value * lax.rsqrt(mean + 1e-6) * bias_mid[1]
-        normed = scaled / (1.0 + jnp.exp(-scaled)) * mask_at(frame, row_base - 2 + row)
+        scaled = value * lax.rsqrt(mean + 1e-6) * bias_of(MID, MID)
+        normed = scaled / (1.0 + jnp.exp(-scaled)) * mask_at(frame, row + 1)
         for tap, moved in enumerate(shifts(normed)):
             norm_cols[at, pl.ds(tap * MID, MID), :] = moved.astype(BF)
         return carry
 
     lax.fori_loop(0, FRAMES * 8, norm_row, 0)
-
-    loads[1].wait()
-
-    def two(phase, taps):
-        return (taps[0], taps[1] + taps[2]) if phase == 0 else (taps[0] + taps[1], taps[2])
-
-    def combine(at, carry):
-        base = pl.multiple_of(at * 16, 16)
-        whole = [
-            [w_up[3 * d + e, pl.ds(base, 16), :].astype(F32) for e in range(3)] for d in range(3)
-        ]
-        for pr in range(2):
-            rows = [two(pr, [whole[d][e] for d in range(3)]) for e in range(3)]
-            for dr in range(2):
-                for pc in range(2):
-                    cells = two(pc, [rows[e][dr] for e in range(3)])
-                    for dc in range(2):
-                        w_phase[2 * pr + pc, pl.ds(base, 16), pl.ds((2 * dr + dc) * MID, MID)] = (
-                            cells[dc].astype(BF)
-                        )
-        return carry
-
-    lax.fori_loop(0, OUT // 16, combine, 0)
 
     loads[2].wait()
 
@@ -176,7 +237,7 @@
             summed = jnp.dot(jnp.concatenate(weights, axis=1), data, preferred_element_type=F32)
             for k in range(2):
                 value = first[frame * 8 + 2 * pair + k + 1].astype(F32) + (
-                    summed[:, k * COLS : (k + 1) * COLS] + bias_mid[2]
+                    summed[:, k * COLS : (k + 1) * COLS] + bias_of(2 * MID, MID)
                 )
                 block[frame * 6 + 2 * pair + k] = value.astype(BF)
         return carry
@@ -198,11 +259,11 @@
             weight = jnp.concatenate([w_time[tap - 1] for tap, _ in taps], axis=1)
             summed = jnp.dot(weight, data, preferred_element_type=F32)
             for k in range(2):
-                row_mask = mask_at(frame, row_base - 1 + 2 * pair + k)
+                row_mask = mask_at(frame, 2 * pair + k + 2)
                 for half in range(2):
                     value = (
                         summed[half * MID : (half + 1) * MID, k * COLS : (k + 1) * COLS]
-                        + bias_time[pl.ds(half * MID, MID), :]
+                        + bias_of((3 + half) * MID, MID)
                     ) * row_mask
                     at = (2 * frame + half) * 6 + 2 * pair + k
                     for tap, moved in enumerate(shifts(value)):
@@ -246,10 +307,10 @@
                         jnp.dot(w_phase[2 * pr + pc], data, preferred_element_type=F32)
                     )
                 for k in range(2):
-                    row_mask = mask_at(frame // 2, row_base + 2 * pair + k)
+                    row_mask = mask_at(frame // 2, 2 * pair + k + 3)
                     mixed = jnp.concatenate(
                         [
-                            ((d[:, k * COLS : (k + 1) * COLS] + bias_up[...]) * row_mask).astype(BF)
+                            ((d[:, k * COLS : (k + 1) * COLS] + bias_of(5 * MID, OUT)) * row_mask).astype(BF)
                             for d in done
                         ],
                         axis=1,
@@ -267,51 +328,50 @@
         out_copy(frame, slot).start()
         return carry
 
+    loads[4].wait()
     lax.fori_loop(0, 2 * FRAMES, up_frame, 0)
     out_copy(2, 0).wait()
     out_copy(3, 1).wait()
 
 
-def decode(info, rims, vectors, weights):
-    hbm = pl.BlockSpec(memory_space=pl.ANY)
+def decode(masks, rims, weights):
+    hbm = pl.BlockSpec(memory_space=pltpu.HBM)
+    anywhere = pl.BlockSpec(memory_space=pl.ANY)
     vmem = pl.BlockSpec(memory_space=pltpu.VMEM)
     return pl.pallas_call(
         decode_kernel,
         out_shape=jax.ShapeDtypeStruct((OUT, 2 * FRAMES, 2 * ROWS, 2 * COLS), BF),
-        in_specs=[pl.BlockSpec(memory_space=pltpu.SMEM)] + [vmem] * 9 + [hbm] * 4,
+        in_specs=[vmem] * 5 + [anywhere] + [hbm] * 3 + [anywhere],
         out_specs=hbm,
         scratch_shapes=[
             pltpu.VMEM((27 * LAT, MID), BF),
             pltpu.VMEM((18, MID, MID), BF),
             pltpu.VMEM((2, 2 * MID, MID), BF),
-            pltpu.VMEM((9, OUT, MID), BF),
+            pltpu.VMEM((4, OUT, 4 * MID), BF),
+            pltpu.VMEM((5 * MID + OUT, COLS), F32),
             pltpu.VMEM((FRAMES, 10, 3 * LAT, COLS), BF),
             pltpu.VMEM((FRAMES * 8, MID, COLS), F32),
             pltpu.VMEM((FRAMES * 8, MID, COLS), BF),
             pltpu.VMEM((FRAMES * 8, 3 * MID, COLS), BF),
             pltpu.VMEM((FRAMES * 6, MID, COLS), BF),
             pltpu.VMEM((2 * FRAMES * 6, 3 * MID, COLS), BF),
-            pltpu.VMEM((4, OUT, 4 * MID), BF),
-            pltpu.VMEM((3, MID, COLS), F32),
-            pltpu.VMEM((2 * MID, COLS), F32),
-            pltpu.VMEM((OUT, COLS), F32),
             pltpu.VMEM((2 * COLS, 2 * COLS), BF),
             pltpu.VMEM((2, OUT * 8, COLS), F32),
             pltpu.VMEM((2, OUT, 8, 2 * COLS), BF),
-            pltpu.SemaphoreType.DMA((4,)),
+            pltpu.SemaphoreType.DMA((5,)),
             pltpu.SemaphoreType.DMA((2,)),
         ],
-        compiler_params=pltpu.CompilerParams(vmem_limit_bytes=44 << 20),
+        compiler_params=pltpu.CompilerParams(vmem_limit_bytes=61 << 20),
         cost_estimate=pl.CostEstimate(
             flops=13_000_000_000, bytes_accessed=13_000_000, transcendentals=800_000
         ),
-    )(info, *rims, *vectors, *weights)
-
-
-def pick(options, chosen):
+    )(masks, *rims, *weights)
+
+
+def pick(options, masks, base):
     result = options[0]
     for k in range(1, len(options)):
-        result = jnp.where(chosen == k, options[k], result)
+        result = jnp.where(masks[base + k] > 0.5, options[k], result)
     return result
 
 
@@ -331,9 +391,10 @@
     w_up,
     b_up,
 ):
-    group, tile = lax.axis_index("req"), lax.axis_index("tile")
-    ring = 4
-    along_x, along_z = group // ring, group % ring
+    ring = RING
+    masks = make_masks(piece_dest, frames, heights, widths)
+    w_up = w_up.reshape(9, OUT, MID)
+    w_phase, bias = prepare((b_in, gain_norm, b_res, b_time, b_up), w_up)
 
     def shift_x(value, k):
         return lax.ppermute(
@@ -349,23 +410,12 @@
             [(x * ring + z, x * ring + (z + k) % ring) for x in range(ring) for z in range(ring)],
         )
 
-    wanted = piece_dest.reshape(ring * ring, -1)[:, 0] // (FRAMES * 32)
     held = [latents] + [shift_x(latents, k) for k in range(1, ring)]
-    held_for = [wanted[(along_x - k) % ring * ring + along_z] for k in range(ring)]
-
-    def select_for(target):
-        chosen = jnp.int32(0)
-        for k in range(1, ring):
-            chosen = jnp.where(held_for[k] == target, k, chosen)
-        return pick(held, chosen)
-
-    arrived = [select_for(group)]
-    for k in range(1, ring):
-        arrived.append(shift_z(select_for(along_x * ring + (along_z + k) % ring), k))
-    source = jnp.argmax(wanted == group).astype(jnp.int32)
-    mine = pick(arrived, (along_z - source % ring) % ring)
-
-    late = tile >= 4
+    picked = [pick(held, masks, PICK_Z + ring * k) for k in range(ring)]
+    arrived = [picked[0]] + [shift_z(picked[k], k) for k in range(1, ring)]
+    mine = pick(arrived, masks, PICK_MINE)
+
+    late = masks[LATE] > 0.5
     upper, lower = mine[0:7], mine[1:8]
     head, tail = mine[0:3], mine[5:8]
     quarter = range(4)
@@ -393,17 +443,14 @@
             + [(4 + s, 2 * s - 1) for s in quarter if s > 0],
         ),
     ]
-    info = jnp.stack(
-        [tile % 2, frames[group], heights[group], widths[group], tile * ROWS]
-    ).astype(jnp.int32)
-    vectors = [v.reshape(1, -1) for v in (b_in, gain_norm, b_res, b_time, b_up)]
     weights = [
+        bias,
         jnp.swapaxes(w_in, 3, 4).reshape(27 * LAT, MID),
         w_res.reshape(27, MID, MID),
         w_time,
-        w_up.reshape(9, OUT, MID),
+        w_phase,
     ]
-    return decode(info, rims, vectors, weights)[None]
+    return decode(masks, rims, weights)[None]
 
 
 def solution(mesh):

time: 74.9 us -> 59.8 us (0.80)
  local copies, waits for them, and re-layouts: 14.4 us -> 0.6 us
  between operations: 9.75 us -> 0.13 us
  Pallas kernels: 25.9 us -> 31.3 us
  waiting for transfers between devices: 0.03 us -> 3.15 us
    pallas_call x0 -> x2, Pallas kernels: none -> 5.44 us  [the longest x1 3.92 us: prepare(): pl.pallas_call(prepare_kernel, out_shape=(jax.ShapeDtypeStruct((4, OUT, 4...]
    dynamic_slice x4 -> x0, local copies, waits for them, and re-layouts: 4.4 us -> none  [the longest x1 1.32 us: on_device(): widths[group]]
    unnamed x8, local copies, waits for them, and re-layouts: 4.45 us -> 0.6 us
    reshape x5 -> x0, local copies, waits for them, and re-layouts: 3.49 us -> none  [the longest x4 2.74 us: on_device(): vectors = [v.reshape(1, -1) for v in (b_in, gain_norm, b_res, b_time, b_up)]]
    ppermute x3, waiting for transfers between devices: 0.01 us -> 2.9 us  [shift_z(): lax.ppermute(value, 'req', [(x * ring + z, x * ring + (z + k) % ring) for...]
    another operation x1 -> x0, local copies, waits for them, and re-layouts: 1.95 us -> none  [on_device(): jnp.stack([tile % 2, frames[group], heights[group], widths[group], tile *...]
    gt x0 -> x1, other arithmetic: none -> 0.92 us  [pick(): result = jnp.where(masks[base + k] > 0.5, options[k], result)]
    select_n x3 -> x2, other arithmetic: 1.57 us -> 1.56 us  [pick(): result = jnp.where(masks[base + k] > 0.5, options[k], result)]
  transfers between devices with their start and end apart: 10 -> 10, of which waited for: 0 -> 3; matrix products, arithmetic and copies ran while one was open for 15% -> 2% of each run, Pallas kernels for 0% -> 9%
where the time goes in v2:
time: 59.8 us; the launch traced here: 58.9 us
  Pallas kernels  31.3 us (52%)
  starting transfers between devices  21.2 us (35%)
  waiting for transfers between devices  3.15 us (5%)
  other arithmetic  2.5 us (4%)
  local copies, waits for them, and re-layouts  0.6 us (1%)
    pallas_call x1, Pallas kernels, decode(): pl.pallas_call(decode_kernel, out_shape=jax.ShapeDtypeStruct((OUT, 2 * FR...  25.9 us
    ppermute x3, starting transfers between devices, shift_z(): lax.ppermute(value, 'req', [(x * ring + z, x * ring + (z + k) % ring) for...  6.58 us
    ppermute x3, starting transfers between devices, shift_x(): lax.ppermute(value, 'req', [(x * ring + z, (x + k) % ring * ring + z) for...  5.65 us
    pallas_call x1, Pallas kernels, prepare(): pl.pallas_call(prepare_kernel, out_shape=(jax.ShapeDtypeStruct((4, OUT, 4...  3.92 us
    ppermute x1, starting transfers between devices, on_device(): lax.ppermute(jnp.where(late, lower, upper), 'tile', [(s, 2 * s) for s in...  3.8 us
    ppermute x1, starting transfers between devices, on_device(): lax.ppermute(jnp.where(late, head, tail), 'tile', [(s, 2 * s + 2) for s i...  3.2 us
    ppermute x3, waiting for transfers between devices, shift_z(): lax.ppermute(value, 'req', [(x * ring + z, x * ring + (z + k) % ring) for...  2.9 us
    ppermute x1, starting transfers between devices, on_device(): lax.ppermute(jnp.where(late, tail, head), 'tile', [(s, 2 * s - 1) for s i...  1.92 us
  transfers between devices with their start and end apart: 10, of which 3 were waited for; matrix products, arithmetic and copies ran while one was open for 2% of the time, Pallas kernels for 9%

profile of v2, /device:TPU:8, one launch (start us, length us, event | category | flops | bytes accessed | tf_op | source)
XLA Modules:
  0.0 58.9 jit_solution(6394139771128686578)
XLA Ops:
  0.0 1.5 %collective-permute-start.2 = (bf16[8,16,128]{2,1,0:T(8,128)(2,1)}, bf16[8,16,128]{2,1,0:T(8,128)(2,1)S(1)}, u32[]{:S(2)}, u32[]{:S(2)}) collective-permute-start(bf16[8,16,128]{2,1,0:T(8,128)(2,1)} %param.14), channel_id=1, source_target_pairs={{0,32},{8,40},{16,48},{24,56},{32,64},{40,72},{48,80},{56,88},{64,... | collective-permute-start | bytes 98312 | tf_op jit(solution)/shard_map/ppermute | solution.py:400
  1.5 2.7 %collective-permute-start.1 = (bf16[8,16,128]{2,1,0:T(8,128)(2,1)}, bf16[8,16,128]{2,1,0:T(8,128)(2,1)S(1)}, u32[]{:S(2)}, u32[]{:S(2)}) collective-permute-start(bf16[8,16,128]{2,1,0:T(8,128)(2,1)} %param.14), channel_id=1, source_target_pairs={{0,64},{8,72},{16,80},{24,88},{32,96},{40,104},{48,112},{56,120},{... | collective-permute-start | bytes 98312 | tf_op jit(solution)/shard_map/ppermute | solution.py:400
  4.2 1.4 %collective-permute-start = (bf16[8,16,128]{2,1,0:T(8,128)(2,1)}, bf16[8,16,128]{2,1,0:T(8,128)(2,1)S(1)}, u32[]{:S(2)}, u32[]{:S(2)}) collective-permute-start(bf16[8,16,128]{2,1,0:T(8,128)(2,1)} %param.14), channel_id=1, source_target_pairs={{0,96},{8,104},{16,112},{24,120},{32,0},{40,8},{48,16},{56,24},{64... | collective-permute-start | bytes 98312 | tf_op jit(solution)/shard_map/ppermute | solution.py:400
  5.7 1.5 %shard_map.136.masks = f32[48,128]{1,0:T(8,128)} custom-call(s32[1024]{0:T(1024)} %piece_dest.1, s32[16]{0:T(128)} %frames.1, s32[16]{0:T(128)} %heights.1, s32[16]{0:T(128)} %widths.1), custom_call_target="tpu_custom_call" | custom-call | flops 100000 | bytes 30000 | tf_op jit(solution)/shard_map/pallas_call | solution.py:76
  7.2 0.9 %compare_bitcast_fusion.14 = (pred[128]{0:T(512)(128)(4,1)S(1)}, pred[128]{0:T(512)(128)(4,1)S(1)}, pred[128]{0:T(512)(128)(4,1)S(1)}, pred[128]{0:T(512)(128)(4...) fusion(f32[48,128]{1,0:T(8,128)} %shard_map.136.masks), kind=kLoop, calls=%fused_computation.22 | loop fusion | flops 2048 | bytes 10240 | tf_op jit(solution)/shard_map/gt | solution.py:374
  8.1 0.0 collective-permute-done.2
  8.1 0.2 collective-permute-done
  8.3 0.8 %select_select_fusion.1 = (bf16[8,16,128]{2,1,0:T(8,128)(2,1)S(1)}, bf16[8,16,128]{2,1,0:T(8,128)(2,1)S(1)}, bf16[8,16,128]{2,1,0:T(8,128)(2,1)S(1)}) fusion(bf16[8,16,128]{2,1,0:T(8,128)(2,1)S(1)} %collective-permute-done, bf16[8,16,128]{2,1,0:T(8,128)(2,1)S(1)} %collective-permute-done.1, bf16[8,16,128]{2,1,0:T(8,128)(2,1)S(1)} %collective-permute-done.2, ...), kind=kLoop, calls=%fused_computation.1 | loop fusion | flops 147456 | bytes 230528 | tf_op jit(solution)/shard_map/jit(_where)/select_n | solution.py:374
  9.1 2.0 %collective-permute-start.5 = (bf16[8,16,128]{2,1,0:T(8,128)(2,1)S(1)}, bf16[8,16,128]{2,1,0:T(8,128)(2,1)S(1)}, u32[]{:S(2)}, u32[]{:S(2)}) collective-permute-start(bf16[8,16,128]{2,1,0:T(8,128)(2,1)S(1)} %get-tuple-element.9), channel_id=1, source_target_pairs={{0,8},{8,16},{16,24},{24,0},{32,40},{40,48},{48,56},{56,32},{64,72... | collective-permute-start | bytes 98312 | tf_op jit(solution)/shard_map/ppermute | solution.py:407
  11.1 3.6 %collective-permute-start.4 = (bf16[8,16,128]{2,1,0:T(8,128)(2,1)S(1)}, bf16[8,16,128]{2,1,0:T(8,128)(2,1)S(1)}, u32[]{:S(2)}, u32[]{:S(2)}) collective-permute-start(bf16[8,16,128]{2,1,0:T(8,128)(2,1)S(1)} %get-tuple-element.10), channel_id=1, source_target_pairs={{0,16},{8,24},{16,0},{24,8},{32,48},{40,56},{48,32},{56,40},{64,80... | collective-permute-start | bytes 98312 | tf_op jit(solution)/shard_map/ppermute | solution.py:407
  14.7 1.0 %collective-permute-start.3 = (bf16[8,16,128]{2,1,0:T(8,128)(2,1)S(1)}, bf16[8,16,128]{2,1,0:T(8,128)(2,1)S(1)}, u32[]{:S(2)}, u32[]{:S(2)}) collective-permute-start(bf16[8,16,128]{2,1,0:T(8,128)(2,1)S(1)} %get-tuple-element.11), channel_id=1, source_target_pairs={{0,24},{8,0},{16,8},{24,16},{32,56},{40,32},{48,40},{56,48},{64,88... | collective-permute-start | bytes 98312 | tf_op jit(solution)/shard_map/ppermute | solution.py:407
  15.7 1.2 %collective-permute-done.4 = bf16[8,16,128]{2,1,0:T(8,128)(2,1)S(1)} collective-permute-done((bf16[8,16,128]{2,1,0:T(8,128)(2,1)S(1)}, bf16[8,16,128]{2,1,0:T(8,128)(2,1)S(1)}, u32[]{:S(2)}, u32[]{:S(2)}) %collective-permute-start.4) | collective-permute-done | bytes 32800 | tf_op jit(solution)/shard_map/ppermute | solution.py:407
  16.9 1.7 %collective-permute-done.3 = bf16[8,16,128]{2,1,0:T(8,128)(2,1)S(1)} collective-permute-done((bf16[8,16,128]{2,1,0:T(8,128)(2,1)S(1)}, bf16[8,16,128]{2,1,0:T(8,128)(2,1)S(1)}, u32[]{:S(2)}, u32[]{:S(2)}) %collective-permute-start.3) | collective-permute-done | bytes 32800 | tf_op jit(solution)/shard_map/ppermute | solution.py:407
  18.6 0.8 %select_select_fusion = bf16[8,16,128]{2,1,0:T(8,128)(2,1)S(1)} fusion(bf16[8,16,128]{2,1,0:T(8,128)(2,1)S(1)} %collective-permute-done.3, bf16[8,16,128]{2,1,0:T(8,128)(2,1)S(1)} %collective-permute-done.4, bf16[8,16,128]{2,1,0:T(8,128)(2,1)S(1)} %collective-permute-done.5, bf16[8,16,128]{2,1,0:T(8,128)(2,1)S(1)} %collective-permute-done, ...), kind=kLoop, calls=%fused_computation | loop fusion | flops 98304 | bytes 262912 | tf_op jit(solution)/shard_map/jit(_where)/select_n | solution.py:374
  19.4 0.1 collective-permute-start.7
  19.5 3.8 %collective-permute-start.6 = (bf16[7,16,128]{2,1,0:T(8,128)(2,1)S(1)}, bf16[7,16,128]{2,1,0:T(8,128)(2,1)S(1)}, u32[]{:S(2)}, u32[]{:S(2)}) collective-permute-start(bf16[7,16,128]{2,1,0:T(8,128)(2,1)S(1)} %get-tuple-element.15), channel_id=1, source_target_pairs={{0,0},{1,2},{2,4},{3,6},{4,1},{5,3},{6,5},{7,7},{8,8},{9,10},{10,1... | collective-permute-start | bytes 86024 | tf_op jit(solution)/shard_map/ppermute | solution.py:423
  23.3 3.2 %collective-permute-start.9 = (bf16[3,16,128]{2,1,0:T(8,128)(2,1)S(1)}, bf16[3,16,128]{2,1,0:T(8,128)(2,1)S(1)}, u32[]{:S(2)}, u32[]{:S(2)}) collective-permute-start(bf16[3,16,128]{2,1,0:T(8,128)(2,1)S(1)} %get-tuple-element.12), channel_id=1, source_target_pairs={{0,2},{1,4},{2,6},{5,1},{6,3},{7,5},{8,10},{9,12},{10,14},{13,9},{... | collective-permute-start | bytes 36872 | tf_op jit(solution)/shard_map/ppermute | solution.py:439
  26.5 1.9 %collective-permute-start.8 = (bf16[3,16,128]{2,1,0:T(8,128)(2,1)S(1)}, bf16[3,16,128]{2,1,0:T(8,128)(2,1)S(1)}, u32[]{:S(2)}, u32[]{:S(2)}) collective-permute-start(bf16[3,16,128]{2,1,0:T(8,128)(2,1)S(1)} %get-tuple-element.13), channel_id=1, source_target_pairs={{1,1},{2,3},{3,5},{4,2},{5,4},{6,6},{9,9},{10,11},{11,13},{12,10},... | collective-permute-start | bytes 36872 | tf_op jit(solution)/shard_map/ppermute | solution.py:433
  28.5 3.9 %shard_map.137 = (bf16[4,192,1536]{2,1,0:T(8,128)(2,1)}, f32[2112,128]{1,0:T(8,128)}) custom-call(f32[384]{0:T(512)} %b_in.1, f32[384]{0:T(512)} %gain.1, f32[384]{0:T(512)} %b_res.1, f32[768]{0:T(1024)} %b_time.1, f32[192]{0:T(256)} %b_up.1, bf16[9,192,384]{2,1,0:T(8,128)(2,1)} %bitcast.38), custom_call_target="tpu_custom_call" | custom-call | flops 10000000 | bytes 5000000 | tf_op jit(solution)/shard_map/pallas_call | solution.py:115
  32.5 0.5 copy-done.2
  33.0 0.0 copy-done.3
  33.0 0.0 copy-done
  33.0 0.0 copy-done.1
  33.0 25.9 %shard_map.138 = bf16[192,4,8,256]{3,2,1,0:T(8,128)(2,1)} custom-call(f32[48,128]{1,0:T(8,128)} %shard_map.136.masks, bf16[7,16,128]{2,1,0:T(8,128)(2,1)} %copy-done.1, bf16[7,16,128]{2,1,0:T(8,128)(2,1)} %copy-done, bf16[3,16,128]{2,1,0:T(8,128)(2,1)} %copy-done.3, bf16[3,16,128]{2,1,0:T(8,128)(2,1)} %copy-done.2, f32[2112,128]{1,0:T(8,128)} %get-tuple-element.7.bias_hbm, ...), custom_call_target="tpu_custom_call" | custom-call | flops 12999999488 | bytes 13000000 | tf_op jit(solution)/shard_map/pallas_call | solution.py:341
  (12 shorter events, 0.0 us)
Async XLA Ops:
  0.0 8.1 %collective-permute-start.2 = (bf16[8,16,128]{2,1,0:T(8,128)(2,1)}, bf16[8,16,128]{2,1,0:T(8,128)(2,1)S(1)}, u32[]{:S(2)}, u32[]{:S(2)}) collective-permute-start(bf16[8,16,128]{2,1,0:T(8,128)(2,1)} %param.14), channel_id=1, source_target_pairs={{0,32},{8,40},{16,48},{24,56},{32,64},{40,72},{48,80},{56,88},{64,... | collective-permute-start | bytes 98312 | tf_op jit(solution)/shard_map/ppermute | solution.py:400
  1.5 6.6 %collective-permute-start.1 = (bf16[8,16,128]{2,1,0:T(8,128)(2,1)}, bf16[8,16,128]{2,1,0:T(8,128)(2,1)S(1)}, u32[]{:S(2)}, u32[]{:S(2)}) collective-permute-start(bf16[8,16,128]{2,1,0:T(8,128)(2,1)} %param.14), channel_id=1, source_target_pairs={{0,64},{8,72},{16,80},{24,88},{32,96},{40,104},{48,112},{56,120},{... | collective-permute-start | bytes 98312 | tf_op jit(solution)/shard_map/ppermute | solution.py:400
  4.2 4.1 %collective-permute-start = (bf16[8,16,128]{2,1,0:T(8,128)(2,1)}, bf16[8,16,128]{2,1,0:T(8,128)(2,1)S(1)}, u32[]{:S(2)}, u32[]{:S(2)}) collective-permute-start(bf16[8,16,128]{2,1,0:T(8,128)(2,1)} %param.14), channel_id=1, source_target_pairs={{0,96},{8,104},{16,112},{24,120},{32,0},{40,8},{48,16},{56,24},{64... | collective-permute-start | bytes 98312 | tf_op jit(solution)/shard_map/ppermute | solution.py:400
  9.1 6.6 %collective-permute-start.5 = (bf16[8,16,128]{2,1,0:T(8,128)(2,1)S(1)}, bf16[8,16,128]{2,1,0:T(8,128)(2,1)S(1)}, u32[]{:S(2)}, u32[]{:S(2)}) collective-permute-start(bf16[8,16,128]{2,1,0:T(8,128)(2,1)S(1)} %get-tuple-element.9), channel_id=1, source_target_pairs={{0,8},{8,16},{16,24},{24,0},{32,40},{40,48},{48,56},{56,32},{64,72... | collective-permute-start | bytes 98312 | tf_op jit(solution)/shard_map/ppermute | solution.py:407
  11.1 5.8 %collective-permute-start.4 = (bf16[8,16,128]{2,1,0:T(8,128)(2,1)S(1)}, bf16[8,16,128]{2,1,0:T(8,128)(2,1)S(1)}, u32[]{:S(2)}, u32[]{:S(2)}) collective-permute-start(bf16[8,16,128]{2,1,0:T(8,128)(2,1)S(1)} %get-tuple-element.10), channel_id=1, source_target_pairs={{0,16},{8,24},{16,0},{24,8},{32,48},{40,56},{48,32},{56,40},{64,80... | collective-permute-start | bytes 98312 | tf_op jit(solution)/shard_map/ppermute | solution.py:407
  14.7 3.9 %collective-permute-start.3 = (bf16[8,16,128]{2,1,0:T(8,128)(2,1)S(1)}, bf16[8,16,128]{2,1,0:T(8,128)(2,1)S(1)}, u32[]{:S(2)}, u32[]{:S(2)}) collective-permute-start(bf16[8,16,128]{2,1,0:T(8,128)(2,1)S(1)} %get-tuple-element.11), channel_id=1, source_target_pairs={{0,24},{8,0},{16,8},{24,16},{32,56},{40,32},{48,40},{56,48},{64,88... | collective-permute-start | bytes 98312 | tf_op jit(solution)/shard_map/ppermute | solution.py:407
  19.4 13.0 %collective-permute-start.7 = (bf16[7,16,128]{2,1,0:T(8,128)(2,1)S(1)}, bf16[7,16,128]{2,1,0:T(8,128)(2,1)S(1)}, u32[]{:S(2)}, u32[]{:S(2)}) collective-permute-start(bf16[7,16,128]{2,1,0:T(8,128)(2,1)S(1)} %get-tuple-element.14), channel_id=1, source_target_pairs={{0,1},{1,3},{2,5},{3,7},{4,0},{5,2},{6,4},{7,6},{8,9},{9,11},{10,1... | collective-permute-start | bytes 86024 | tf_op jit(solution)/shard_map/ppermute | solution.py:428
  19.5 12.9 %collective-permute-start.6 = (bf16[7,16,128]{2,1,0:T(8,128)(2,1)S(1)}, bf16[7,16,128]{2,1,0:T(8,128)(2,1)S(1)}, u32[]{:S(2)}, u32[]{:S(2)}) collective-permute-start(bf16[7,16,128]{2,1,0:T(8,128)(2,1)S(1)} %get-tuple-element.15), channel_id=1, source_target_pairs={{0,0},{1,2},{2,4},{3,6},{4,1},{5,3},{6,5},{7,7},{8,8},{9,10},{10,1... | collective-permute-start | bytes 86024 | tf_op jit(solution)/shard_map/ppermute | solution.py:423
  23.3 9.1 %collective-permute-start.9 = (bf16[3,16,128]{2,1,0:T(8,128)(2,1)S(1)}, bf16[3,16,128]{2,1,0:T(8,128)(2,1)S(1)}, u32[]{:S(2)}, u32[]{:S(2)}) collective-permute-start(bf16[3,16,128]{2,1,0:T(8,128)(2,1)S(1)} %get-tuple-element.12), channel_id=1, source_target_pairs={{0,2},{1,4},{2,6},{5,1},{6,3},{7,5},{8,10},{9,12},{10,14},{13,9},{... | collective-permute-start | bytes 36872 | tf_op jit(solution)/shard_map/ppermute | solution.py:439
  26.5 5.9 %collective-permute-start.8 = (bf16[3,16,128]{2,1,0:T(8,128)(2,1)S(1)}, bf16[3,16,128]{2,1,0:T(8,128)(2,1)S(1)}, u32[]{:S(2)}, u32[]{:S(2)}) collective-permute-start(bf16[3,16,128]{2,1,0:T(8,128)(2,1)S(1)} %get-tuple-element.13), channel_id=1, source_target_pairs={{1,1},{2,3},{3,5},{4,2},{5,4},{6,6},{9,9},{10,11},{11,13},{12,10},... | collective-permute-start | bytes 36872 | tf_op jit(solution)/shard_map/ppermute | solution.py:433
  32.4 0.6 %copy-start.2 = (bf16[3,16,128]{2,1,0:T(8,128)(2,1)}, bf16[3,16,128]{2,1,0:T(8,128)(2,1)S(1)}, u32[]{:S(2)}) copy-start(bf16[3,16,128]{2,1,0:T(8,128)(2,1)S(1)} %collective-permute-done.9.rim_d) | copy-start | bytes 36868
  32.4 0.6 %copy-start.3 = (bf16[3,16,128]{2,1,0:T(8,128)(2,1)}, bf16[3,16,128]{2,1,0:T(8,128)(2,1)S(1)}, u32[]{:S(2)}) copy-start(bf16[3,16,128]{2,1,0:T(8,128)(2,1)S(1)} %collective-permute-done.8.rim_c) | copy-start | bytes 36868
  32.4 0.6 %copy-start = (bf16[7,16,128]{2,1,0:T(8,128)(2,1)}, bf16[7,16,128]{2,1,0:T(8,128)(2,1)S(1)}, u32[]{:S(2)}) copy-start(bf16[7,16,128]{2,1,0:T(8,128)(2,1)S(1)} %collective-permute-done.7.rim_b) | copy-start | bytes 86020
  32.4 0.6 %copy-start.1 = (bf16[7,16,128]{2,1,0:T(8,128)(2,1)}, bf16[7,16,128]{2,1,0:T(8,128)(2,1)S(1)}, u32[]{:S(2)}) copy-start(bf16[7,16,128]{2,1,0:T(8,128)(2,1)S(1)} %collective-permute-done.6.rim_a) | copy-start | bytes 86020

commit v3 on v2

--- a/solution.py
+++ b/solution.py
@@ -27,8 +27,9 @@
 
 def shifts(x):
     col = lax.broadcasted_iota(jnp.int32, x.shape, 1)
-    before = jnp.where(col == 0, 0.0, pltpu.roll(x, 1, 1))
-    after = jnp.where(col == COLS - 1, 0.0, pltpu.roll(x, COLS - 1, 1))
+    zero = jnp.zeros_like(x)
+    before = jnp.where(col == 0, zero, pltpu.roll(x, 1, 1))
+    after = jnp.where(col == COLS - 1, zero, pltpu.roll(x, COLS - 1, 1))
     return before, x, after
 
 
@@ -184,8 +185,8 @@
             other = main_odd[row] if row < 7 else rest_odd[row - 7]
             value = jnp.where(odd, other.astype(F32), even.astype(F32))
             value = value * mask_at(frame, row)
-            for at, moved in enumerate(shifts(value)):
-                lat_cols[frame, row, pl.ds(at * LAT, LAT), :] = moved.astype(BF)
+            for at, moved in enumerate(shifts(value.astype(BF))):
+                lat_cols[frame, row, pl.ds(at * LAT, LAT), :] = moved
 
     loads[0].wait()
     for frame in range(FRAMES):
@@ -214,12 +215,13 @@
         value = value.astype(F32)
         mean = jnp.sum(value * value, axis=0, keepdims=True) * (1.0 / MID)
         scaled = value * lax.rsqrt(mean + 1e-6) * bias_of(MID, MID)
-        normed = scaled / (1.0 + jnp.exp(-scaled)) * mask_at(frame, row + 1)
-        for tap, moved in enumerate(shifts(normed)):
-            norm_cols[at, pl.ds(tap * MID, MID), :] = moved.astype(BF)
+        half = 0.5 * scaled
+        normed = (half + half * jnp.tanh(half)) * mask_at(frame, row + 1)
+        for tap, moved in enumerate(shifts(normed.astype(BF))):
+            norm_cols[at, pl.ds(tap * MID, MID), :] = moved
         return carry
 
-    lax.fori_loop(0, FRAMES * 8, norm_row, 0)
+    lax.fori_loop(0, FRAMES * 8, norm_row, 0, unroll=2)
 
     loads[2].wait()
 
@@ -266,8 +268,8 @@
                         + bias_of((3 + half) * MID, MID)
                     ) * row_mask
                     at = (2 * frame + half) * 6 + 2 * pair + k
-                    for tap, moved in enumerate(shifts(value)):
-                        time_cols[at, pl.ds(tap * MID, MID), :] = moved.astype(BF)
+                    for tap, moved in enumerate(shifts(value.astype(BF))):
+                        time_cols[at, pl.ds(tap * MID, MID), :] = moved
         return carry
 
     lax.fori_loop(0, 3, time_pair, 0)
@@ -394,7 +396,6 @@
     ring = RING
     masks = make_masks(piece_dest, frames, heights, widths)
     w_up = w_up.reshape(9, OUT, MID)
-    w_phase, bias = prepare((b_in, gain_norm, b_res, b_time, b_up), w_up)
 
     def shift_x(value, k):
         return lax.ppermute(
@@ -412,7 +413,11 @@
 
     held = [latents] + [shift_x(latents, k) for k in range(1, ring)]
     picked = [pick(held, masks, PICK_Z + ring * k) for k in range(ring)]
+    first_pick, w_up = lax.optimization_barrier((picked[0], w_up))
+    picked[0] = first_pick
+    w_phase, bias = prepare((b_in, gain_norm, b_res, b_time, b_up), w_up)
     arrived = [picked[0]] + [shift_z(picked[k], k) for k in range(1, ring)]
+    masks, w_phase, bias = lax.optimization_barrier((masks, w_phase, bias))
     mine = pick(arrived, masks, PICK_MINE)
 
     late = masks[LATE] > 0.5

time: 59.8 us -> 59.5 us (level)
  waiting for transfers between devices: 3.15 us -> 5.67 us
  Pallas kernels: 31.3 us -> 29.5 us
  starting transfers between devices: 21.2 us -> 20.6 us
    ppermute x1, waiting for transfers between devices: 0.01 us -> 3.21 us  [on_device(): lax.ppermute(jnp.where(late, tail, head), 'tile', [(s, 2 * s - 1) for s i...]
    ppermute x3, waiting for transfers between devices: 2.9 us -> 0.01 us  [shift_z(): lax.ppermute(value, 'req', [(x * ring + z, x * ring + (z + k) % ring) for...]
    pallas_call x1, Pallas kernels: 25.9 us -> 24.1 us  [decode(): pl.pallas_call(decode_kernel, out_shape=jax.ShapeDtypeStruct((OUT, 2 * FR...]
    ppermute x3, waiting for transfers between devices: 0.23 us -> 2 us  [shift_x(): lax.ppermute(value, 'req', [(x * ring + z, (x + k) % ring * ring + z) for...]
    gt x1 -> x2, other arithmetic: 0.92 us -> 1.75 us  [pick(): result = jnp.where(masks[base + k] > 0.5, options[k], result)]
    select_n x2, other arithmetic: 1.56 us -> 0.8 us  [pick(): result = jnp.where(masks[base + k] > 0.5, options[k], result)]
    ppermute x3, starting transfers between devices: 5.65 us -> 5.05 us  [shift_x(): lax.ppermute(value, 'req', [(x * ring + z, (x + k) % ring * ring + z) for...]
  transfers between devices with their start and end apart: 10 -> 10, of which waited for: 3 -> 3; matrix products, arithmetic and copies ran while one was open for 2% -> 3% of each run, Pallas kernels for 9% -> 9%
where the time goes in v3:
time: 59.5 us; the launch traced here: 59.1 us
  Pallas kernels  29.5 us (50%)
  starting transfers between devices  20.6 us (35%)
  waiting for transfers between devices  5.67 us (10%)
  other arithmetic  2.57 us (4%)
  local copies, waits for them, and re-layouts  0.6 us (1%)
    pallas_call x1, Pallas kernels, decode(): pl.pallas_call(decode_kernel, out_shape=jax.ShapeDtypeStruct((OUT, 2 * FR...  24.1 us
    ppermute x3, starting transfers between devices, shift_z(): lax.ppermute(value, 'req', [(x * ring + z, x * ring + (z + k) % ring) for...  6.58 us
    ppermute x3, starting transfers between devices, shift_x(): lax.ppermute(value, 'req', [(x * ring + z, (x + k) % ring * ring + z) for...  5.05 us
    pallas_call x1, Pallas kernels, prepare(): pl.pallas_call(prepare_kernel, out_shape=(jax.ShapeDtypeStruct((4, OUT, 4...  3.91 us
    ppermute x1, starting transfers between devices, on_device(): lax.ppermute(jnp.where(late, lower, upper), 'tile', [(s, 2 * s) for s in...  3.8 us
    ppermute x1, waiting for transfers between devices, on_device(): lax.ppermute(jnp.where(late, tail, head), 'tile', [(s, 2 * s - 1) for s i...  3.21 us
    ppermute x1, starting transfers between devices, on_device(): lax.ppermute(jnp.where(late, head, tail), 'tile', [(s, 2 * s + 2) for s i...  3.2 us
    ppermute x3, waiting for transfers between devices, shift_x(): lax.ppermute(value, 'req', [(x * ring + z, (x + k) % ring * ring + z) for...  2 us
  transfers between devices with their start and end apart: 10, of which 3 were waited for; matrix products, arithmetic and copies ran while one was open for 3% of the time, Pallas kernels for 9%

profile of v3, /device:TPU:8, one launch (start us, length us, event | category | flops | bytes accessed | tf_op | source)
XLA Modules:
  0.0 59.1 jit_solution(14836470620666287163)
XLA Ops:
  0.0 3.0 %collective-permute-start.1 = (bf16[8,16,128]{2,1,0:T(8,128)(2,1)}, bf16[8,16,128]{2,1,0:T(8,128)(2,1)S(1)}, u32[]{:S(2)}, u32[]{:S(2)}) collective-permute-start(bf16[8,16,128]{2,1,0:T(8,128)(2,1)} %param.14), channel_id=1, source_target_pairs={{0,64},{8,72},{16,80},{24,88},{32,96},{40,104},{48,112},{56,120},{... | collective-permute-start | bytes 98312 | tf_op jit(solution)/shard_map/ppermute | solution.py:401
  3.0 1.1 %collective-permute-start = (bf16[8,16,128]{2,1,0:T(8,128)(2,1)}, bf16[8,16,128]{2,1,0:T(8,128)(2,1)S(1)}, u32[]{:S(2)}, u32[]{:S(2)}) collective-permute-start(bf16[8,16,128]{2,1,0:T(8,128)(2,1)} %param.14), channel_id=1, source_target_pairs={{0,96},{8,104},{16,112},{24,120},{32,0},{40,8},{48,16},{56,24},{64... | collective-permute-start | bytes 98312 | tf_op jit(solution)/shard_map/ppermute | solution.py:401
  4.2 0.9 %collective-permute-start.2 = (bf16[8,16,128]{2,1,0:T(8,128)(2,1)}, bf16[8,16,128]{2,1,0:T(8,128)(2,1)S(1)}, u32[]{:S(2)}, u32[]{:S(2)}) collective-permute-start(bf16[8,16,128]{2,1,0:T(8,128)(2,1)} %param.14), channel_id=1, source_target_pairs={{0,32},{8,40},{16,48},{24,56},{32,64},{40,72},{48,80},{56,88},{64,... | collective-permute-start | bytes 98312 | tf_op jit(solution)/shard_map/ppermute | solution.py:401
  5.1 1.5 %shard_map.136.masks = f32[48,128]{1,0:T(8,128)} custom-call(s32[1024]{0:T(1024)} %piece_dest.1, s32[16]{0:T(128)} %frames.1, s32[16]{0:T(128)} %heights.1, s32[16]{0:T(128)} %widths.1), custom_call_target="tpu_custom_call" | custom-call | flops 100000 | bytes 30000 | tf_op jit(solution)/shard_map/pallas_call | solution.py:77
  6.6 0.9 %compare_bitcast_fusion.2 = (pred[128]{0:T(512)(128)(4,1)S(1)}, pred[128]{0:T(512)(128)(4,1)S(1)}, pred[128]{0:T(512)(128)(4,1)S(1)}, pred[128]{0:T(512)(128)(4,...) fusion(f32[48,128]{1,0:T(8,128)} %shard_map.136.masks), kind=kLoop, calls=%fused_computation.11 | loop fusion | flops 1536 | bytes 7680 | tf_op jit(solution)/shard_map/gt | solution.py:376
  7.5 0.0 collective-permute-done.1
  7.5 2.0 %collective-permute-done.2 = bf16[8,16,128]{2,1,0:T(8,128)(2,1)S(1)} collective-permute-done((bf16[8,16,128]{2,1,0:T(8,128)(2,1)}, bf16[8,16,128]{2,1,0:T(8,128)(2,1)S(1)}, u32[]{:S(2)}, u32[]{:S(2)}) %collective-permute-start.2) | collective-permute-done | bytes 32800 | tf_op jit(solution)/shard_map/ppermute | solution.py:401
  9.5 0.8 %select_select_fusion.1 = (bf16[8,16,128]{2,1,0:T(8,128)(2,1)S(1)}, bf16[8,16,128]{2,1,0:T(8,128)(2,1)S(1)}, bf16[8,16,128]{2,1,0:T(8,128)(2,1)S(1)}, bf16[8,16,128]{2,1,0:T(8,128)(2,1)S(1)}) fusion(bf16[8,16,128]{2,1,0:T(8,128)(2,1)S(1)} %collective-permute-done, bf16[8,16,128]{2,1,0:T(8,128)(2,1)S(1)} %collective-permute-done.1, ...), kind=kLoop, calls=%fused_computation.1 | loop fusion | flops 196608 | bytes 263680 | tf_op jit(solution)/shard_map/jit(_where)/select_n | solution.py:376
  10.3 2.0 %collective-permute-start.5 = (bf16[8,16,128]{2,1,0:T(8,128)(2,1)S(1)}, bf16[8,16,128]{2,1,0:T(8,128)(2,1)S(1)}, u32[]{:S(2)}, u32[]{:S(2)}) collective-permute-start(bf16[8,16,128]{2,1,0:T(8,128)(2,1)S(1)} %get-tuple-element.19), channel_id=1, source_target_pairs={{0,8},{8,16},{16,24},{24,0},{32,40},{40,48},{48,56},{56,32},{64,72... | collective-permute-start | bytes 98312 | tf_op jit(solution)/shard_map/ppermute | solution.py:408
  12.3 3.6 %collective-permute-start.4 = (bf16[8,16,128]{2,1,0:T(8,128)(2,1)S(1)}, bf16[8,16,128]{2,1,0:T(8,128)(2,1)S(1)}, u32[]{:S(2)}, u32[]{:S(2)}) collective-permute-start(bf16[8,16,128]{2,1,0:T(8,128)(2,1)S(1)} %get-tuple-element.20), channel_id=1, source_target_pairs={{0,16},{8,24},{16,0},{24,8},{32,48},{40,56},{48,32},{56,40},{64,80... | collective-permute-start | bytes 98312 | tf_op jit(solution)/shard_map/ppermute | solution.py:408
  15.9 1.0 %collective-permute-start.3 = (bf16[8,16,128]{2,1,0:T(8,128)(2,1)S(1)}, bf16[8,16,128]{2,1,0:T(8,128)(2,1)S(1)}, u32[]{:S(2)}, u32[]{:S(2)}) collective-permute-start(bf16[8,16,128]{2,1,0:T(8,128)(2,1)S(1)} %get-tuple-element.21), channel_id=1, source_target_pairs={{0,24},{8,0},{16,8},{24,16},{32,56},{40,32},{48,40},{56,48},{64,88... | collective-permute-start | bytes 98312 | tf_op jit(solution)/shard_map/ppermute | solution.py:408
  16.9 3.9 %shard_map.137 = (bf16[4,192,1536]{2,1,0:T(8,128)(2,1)}, f32[2112,128]{1,0:T(8,128)}) custom-call(f32[384]{0:T(512)} %b_in.1, f32[384]{0:T(512)} %gain.1, f32[384]{0:T(512)} %b_res.1, f32[768]{0:T(1024)} %b_time.1, f32[192]{0:T(256)} %b_up.1, bf16[9,192,384]{2,1,0:T(8,128)(2,1)} %bitcast.38), custom_call_target="tpu_custom_call" | custom-call | flops 10000000 | bytes 5000000 | tf_op jit(solution)/shard_map/pallas_call | solution.py:116
  20.8 0.8 %compare_bitcast_fusion.11 = (pred[128]{0:T(512)(128)(4,1)S(1)}, pred[128]{0:T(512)(128)(4,1)S(1)}, pred[128]{0:T(512)(128)(4,1)S(1)}, pred[128]{0:T(512)(128)(4,1)S(1)}) fusion(f32[48,128]{1,0:T(8,128)} %shard_map.136.masks), kind=kLoop, calls=%fused_computation.20 | loop fusion | flops 512 | bytes 2560 | tf_op jit(solution)/shard_map/gt | solution.py:376
  21.6 0.0 collective-permute-done.5
  21.7 0.1 collective-permute-start.7
  21.8 3.8 %collective-permute-start.6 = (bf16[7,16,128]{2,1,0:T(8,128)(2,1)S(1)}, bf16[7,16,128]{2,1,0:T(8,128)(2,1)S(1)}, u32[]{:S(2)}, u32[]{:S(2)}) collective-permute-start(bf16[7,16,128]{2,1,0:T(8,128)(2,1)S(1)} %get-tuple-element.26), channel_id=1, source_target_pairs={{0,0},{1,2},{2,4},{3,6},{4,1},{5,3},{6,5},{7,7},{8,8},{9,10},{10,1... | collective-permute-start | bytes 86024 | tf_op jit(solution)/shard_map/ppermute | solution.py:428
  25.6 3.2 %collective-permute-start.9 = (bf16[3,16,128]{2,1,0:T(8,128)(2,1)S(1)}, bf16[3,16,128]{2,1,0:T(8,128)(2,1)S(1)}, u32[]{:S(2)}, u32[]{:S(2)}) collective-permute-start(bf16[3,16,128]{2,1,0:T(8,128)(2,1)S(1)} %get-tuple-element.23), channel_id=1, source_target_pairs={{0,2},{1,4},{2,6},{5,1},{6,3},{7,5},{8,10},{9,12},{10,14},{13,9},{... | collective-permute-start | bytes 36872 | tf_op jit(solution)/shard_map/ppermute | solution.py:444
  28.8 1.9 %collective-permute-start.8 = (bf16[3,16,128]{2,1,0:T(8,128)(2,1)S(1)}, bf16[3,16,128]{2,1,0:T(8,128)(2,1)S(1)}, u32[]{:S(2)}, u32[]{:S(2)}) collective-permute-start(bf16[3,16,128]{2,1,0:T(8,128)(2,1)S(1)} %get-tuple-element.24), channel_id=1, source_target_pairs={{1,1},{2,3},{3,5},{4,2},{5,4},{6,6},{9,9},{10,11},{11,13},{12,10},... | collective-permute-start | bytes 36872 | tf_op jit(solution)/shard_map/ppermute | solution.py:438
  30.7 0.4 collective-permute-done.9.rim_d
  31.2 3.2 %collective-permute-done.8.rim_c = bf16[3,16,128]{2,1,0:T(8,128)(2,1)S(1)} collective-permute-done((bf16[3,16,128]{2,1,0:T(8,128)(2,1)S(1)}, bf16[3,16,128]{2,1,0:T(8,128)(2,1)S(1)}, u32[]{:S(2)}, u32[]{:S(2)}) %collective-permute-start.8) | collective-permute-done | bytes 12320 | tf_op jit(solution)/shard_map/ppermute | solution.py:438
  34.4 0.6 copy-done.3
  35.0 0.0 copy-done
  35.0 0.0 copy-done.1
  35.0 24.1 %shard_map.138 = bf16[192,4,8,256]{3,2,1,0:T(8,128)(2,1)} custom-call(f32[48,128]{1,0:T(8,128)} %shard_map.136.masks, bf16[7,16,128]{2,1,0:T(8,128)(2,1)} %copy-done.1, bf16[7,16,128]{2,1,0:T(8,128)(2,1)} %copy-done, bf16[3,16,128]{2,1,0:T(8,128)(2,1)} %copy-done.3, bf16[3,16,128]{2,1,0:T(8,128)(2,1)} %copy-done.2, f32[2112,128]{1,0:T(8,128)} %get-tuple-element.17.bias_hbm, ...), custom_call_target="tpu_custom_call" | custom-call | flops 12999999488 | bytes 13000000 | tf_op jit(solution)/shard_map/pallas_call | solution.py:343
  (13 shorter events, 0.1 us)
Async XLA Ops:
  0.0 7.5 %collective-permute-start.1 = (bf16[8,16,128]{2,1,0:T(8,128)(2,1)}, bf16[8,16,128]{2,1,0:T(8,128)(2,1)S(1)}, u32[]{:S(2)}, u32[]{:S(2)}) collective-permute-start(bf16[8,16,128]{2,1,0:T(8,128)(2,1)} %param.14), channel_id=1, source_target_pairs={{0,64},{8,72},{16,80},{24,88},{32,96},{40,104},{48,112},{56,120},{... | collective-permute-start | bytes 98312 | tf_op jit(solution)/shard_map/ppermute | solution.py:401
  3.0 4.5 %collective-permute-start = (bf16[8,16,128]{2,1,0:T(8,128)(2,1)}, bf16[8,16,128]{2,1,0:T(8,128)(2,1)S(1)}, u32[]{:S(2)}, u32[]{:S(2)}) collective-permute-start(bf16[8,16,128]{2,1,0:T(8,128)(2,1)} %param.14), channel_id=1, source_target_pairs={{0,96},{8,104},{16,112},{24,120},{32,0},{40,8},{48,16},{56,24},{64... | collective-permute-start | bytes 98312 | tf_op jit(solution)/shard_map/ppermute | solution.py:401
  4.2 5.3 %collective-permute-start.2 = (bf16[8,16,128]{2,1,0:T(8,128)(2,1)}, bf16[8,16,128]{2,1,0:T(8,128)(2,1)S(1)}, u32[]{:S(2)}, u32[]{:S(2)}) collective-permute-start(bf16[8,16,128]{2,1,0:T(8,128)(2,1)} %param.14), channel_id=1, source_target_pairs={{0,32},{8,40},{16,48},{24,56},{32,64},{40,72},{48,80},{56,88},{64,... | collective-permute-start | bytes 98312 | tf_op jit(solution)/shard_map/ppermute | solution.py:401
  10.3 11.3 %collective-permute-start.5 = (bf16[8,16,128]{2,1,0:T(8,128)(2,1)S(1)}, bf16[8,16,128]{2,1,0:T(8,128)(2,1)S(1)}, u32[]{:S(2)}, u32[]{:S(2)}) collective-permute-start(bf16[8,16,128]{2,1,0:T(8,128)(2,1)S(1)} %get-tuple-element.19), channel_id=1, source_target_pairs={{0,8},{8,16},{16,24},{24,0},{32,40},{40,48},{48,56},{56,32},{64,72... | collective-permute-start | bytes 98312 | tf_op jit(solution)/shard_map/ppermute | solution.py:408
  12.3 9.3 %collective-permute-start.4 = (bf16[8,16,128]{2,1,0:T(8,128)(2,1)S(1)}, bf16[8,16,128]{2,1,0:T(8,128)(2,1)S(1)}, u32[]{:S(2)}, u32[]{:S(2)}) collective-permute-start(bf16[8,16,128]{2,1,0:T(8,128)(2,1)S(1)} %get-tuple-element.20), channel_id=1, source_target_pairs={{0,16},{8,24},{16,0},{24,8},{32,48},{40,56},{48,32},{56,40},{64,80... | collective-permute-start | bytes 98312 | tf_op jit(solution)/shard_map/ppermute | solution.py:408
  15.9 5.8 %collective-permute-start.3 = (bf16[8,16,128]{2,1,0:T(8,128)(2,1)S(1)}, bf16[8,16,128]{2,1,0:T(8,128)(2,1)S(1)}, u32[]{:S(2)}, u32[]{:S(2)}) collective-permute-start(bf16[8,16,128]{2,1,0:T(8,128)(2,1)S(1)} %get-tuple-element.21), channel_id=1, source_target_pairs={{0,24},{8,0},{16,8},{24,16},{32,56},{40,32},{48,40},{56,48},{64,88... | collective-permute-start | bytes 98312 | tf_op jit(solution)/shard_map/ppermute | solution.py:408
  21.7 12.7 %collective-permute-start.7 = (bf16[7,16,128]{2,1,0:T(8,128)(2,1)S(1)}, bf16[7,16,128]{2,1,0:T(8,128)(2,1)S(1)}, u32[]{:S(2)}, u32[]{:S(2)}) collective-permute-start(bf16[7,16,128]{2,1,0:T(8,128)(2,1)S(1)} %get-tuple-element.25), channel_id=1, source_target_pairs={{0,1},{1,3},{2,5},{3,7},{4,0},{5,2},{6,4},{7,6},{8,9},{9,11},{10,1... | collective-permute-start | bytes 86024 | tf_op jit(solution)/shard_map/ppermute | solution.py:433
  21.8 12.6 %collective-permute-start.6 = (bf16[7,16,128]{2,1,0:T(8,128)(2,1)S(1)}, bf16[7,16,128]{2,1,0:T(8,128)(2,1)S(1)}, u32[]{:S(2)}, u32[]{:S(2)}) collective-permute-start(bf16[7,16,128]{2,1,0:T(8,128)(2,1)S(1)} %get-tuple-element.26), channel_id=1, source_target_pairs={{0,0},{1,2},{2,4},{3,6},{4,1},{5,3},{6,5},{7,7},{8,8},{9,10},{10,1... | collective-permute-start | bytes 86024 | tf_op jit(solution)/shard_map/ppermute | solution.py:428
  25.6 5.6 %collective-permute-start.9 = (bf16[3,16,128]{2,1,0:T(8,128)(2,1)S(1)}, bf16[3,16,128]{2,1,0:T(8,128)(2,1)S(1)}, u32[]{:S(2)}, u32[]{:S(2)}) collective-permute-start(bf16[3,16,128]{2,1,0:T(8,128)(2,1)S(1)} %get-tuple-element.23), channel_id=1, source_target_pairs={{0,2},{1,4},{2,6},{5,1},{6,3},{7,5},{8,10},{9,12},{10,14},{13,9},{... | collective-permute-start | bytes 36872 | tf_op jit(solution)/shard_map/ppermute | solution.py:444
  28.8 5.6 %collective-permute-start.8 = (bf16[3,16,128]{2,1,0:T(8,128)(2,1)S(1)}, bf16[3,16,128]{2,1,0:T(8,128)(2,1)S(1)}, u32[]{:S(2)}, u32[]{:S(2)}) collective-permute-start(bf16[3,16,128]{2,1,0:T(8,128)(2,1)S(1)} %get-tuple-element.24), channel_id=1, source_target_pairs={{1,1},{2,3},{3,5},{4,2},{5,4},{6,6},{9,9},{10,11},{11,13},{12,10},... | collective-permute-start | bytes 36872 | tf_op jit(solution)/shard_map/ppermute | solution.py:438
  31.2 3.2 %copy-start.2 = (bf16[3,16,128]{2,1,0:T(8,128)(2,1)}, bf16[3,16,128]{2,1,0:T(8,128)(2,1)S(1)}, u32[]{:S(2)}) copy-start(bf16[3,16,128]{2,1,0:T(8,128)(2,1)S(1)} %collective-permute-done.9.rim_d) | copy-start | bytes 36868
  34.4 0.6 %copy-start.3 = (bf16[3,16,128]{2,1,0:T(8,128)(2,1)}, bf16[3,16,128]{2,1,0:T(8,128)(2,1)S(1)}, u32[]{:S(2)}) copy-start(bf16[3,16,128]{2,1,0:T(8,128)(2,1)S(1)} %collective-permute-done.8.rim_c) | copy-start | bytes 36868
  34.4 0.6 %copy-start = (bf16[7,16,128]{2,1,0:T(8,128)(2,1)}, bf16[7,16,128]{2,1,0:T(8,128)(2,1)S(1)}, u32[]{:S(2)}) copy-start(bf16[7,16,128]{2,1,0:T(8,128)(2,1)S(1)} %collective-permute-done.7.rim_b) | copy-start | bytes 86020
  34.4 0.6 %copy-start.1 = (bf16[7,16,128]{2,1,0:T(8,128)(2,1)}, bf16[7,16,128]{2,1,0:T(8,128)(2,1)S(1)}, u32[]{:S(2)}) copy-start(bf16[7,16,128]{2,1,0:T(8,128)(2,1)S(1)} %collective-permute-done.6.rim_a) | copy-start | bytes 86020
